TPU v7x, 32 devices: a whole 2x2x4 slice. The times are simulated.
32 devices in a mesh: grp: 4 (over x, core), ep: 8 (over z, y).
Axes of the slice: x: 2, y: 2, z: 4, core: 2. Of those that a mesh axis runs over, the one named last changes fastest.
Arguments:
- features: bfloat16 [8192, 1152], P(('grp', 'ep')), may hold values from -6 to 6
- token_position: int32 [8192], P(('grp', 'ep')), may hold values from 0 to 2047, as said below
- expert_ids: int32 [8192, 2], P(('grp', 'ep')), may hold values from 0 to 7, all different within a row; in each aligned block of 256 rows (0 to 255, 256 to 511, ...) at most 128 rows name the same one
- proj_in: bfloat16 [1152, 2560], P('ep'), may hold values from -0.1875 to 0.1875
- bias_in: float32 [2560], replicated, may hold values from -3 to 3
- proj_out: bfloat16 [2560, 2560], P('ep'), may hold values from -0.125 to 0.125
- bias_out: float32 [2560], replicated, may hold values from -3 to 3
- norm_gain: float32 [2560], replicated, may hold values from 0.1 to 1.9
- router: bfloat16 [2560, 8], replicated, may hold values from -0.125 to 0.125
- w_gate: bfloat16 [8, 2560, 512], P('ep'), may hold values from -0.125 to 0.125
- w_up: bfloat16 [8, 2560, 512], P('ep'), may hold values from -0.125 to 0.125
- w_down: bfloat16 [8, 512, 2560], P('ep'), may hold values from -0.25 to 0.25
Outputs:
- mixed: bfloat16 [8192, 2560], P(('grp', 'ep'))
Inputs may be any that keep to these rules, and one draw needn't show every extreme that they name: `token_position`: within each group of 8 devices along ep, the group's values form a permutation of 0 to 2047; position q belongs to the device of ep index q // 256. The rows of each device hold exactly 32 positions of every device of its group. `expert_ids`: each row names 2 different experts; no expert is named by more than 128 of the rows of one device.
All inputs are finite; a program needn't handle non-finite values.
Results may differ from a plain program's by a relative error of at most 0.0071.
Values may be sent and summed in bfloat16 or wider, within the bound.
A program may use at most 192 MiB of HBM per device.

v0:
```python
import jax
import jax.numpy as jnp
from jax import lax
from jax.sharding import PartitionSpec as P

EPSILON = 1e-06


def project(patches, proj_in, bias_in, proj_out, bias_out):
    first_full = lax.all_gather(proj_in, "ep", axis=0, tiled=True)
    pre_act = jnp.dot(patches, first_full, preferred_element_type=jnp.float32)
    hidden = jax.nn.gelu(pre_act + bias_in, approximate=False).astype(jnp.bfloat16)
    second_full = lax.all_gather(proj_out, "ep", axis=0, tiled=True)
    result = jnp.dot(hidden, second_full, preferred_element_type=jnp.float32)
    return (result + bias_out).astype(jnp.bfloat16)


def shards(
    features,
    token_position,
    expert_ids,
    proj_in,
    bias_in,
    proj_out,
    bias_out,
    norm_gain,
    router,
    w_gate,
    w_up,
    w_down,
):
    members = lax.axis_size("ep")
    own_index = lax.axis_index("ep")
    row_count = features.shape[0]
    per_peer = row_count // members
    sender_order = jnp.argsort(token_position, stable=True)
    whole_map = lax.all_gather(token_position, "ep", axis=0, tiled=True).reshape(members, row_count)
    arriving = whole_map // row_count == own_index
    landing_key = jnp.where(arriving, whole_map % row_count, row_count)
    landing = jnp.sort(landing_key, axis=1)[:, :per_peer].reshape(row_count)
    placement_order = jnp.argsort(landing)
    arrived = lax.all_to_all(features[sender_order], "ep", split_axis=0, concat_axis=0, tiled=True)
    tokens = project(arrived[placement_order], proj_in, bias_in, proj_out, bias_out)
    width = tokens.shape[1]
    wide = tokens.astype(jnp.float32)
    scale = lax.rsqrt(jnp.mean(wide * wide, axis=-1, keepdims=True) + EPSILON)
    normed = (wide * scale * norm_gain).astype(jnp.bfloat16)
    experts = router.shape[1]
    top_count = expert_ids.shape[1]
    capacity = 2 * row_count * top_count // experts
    local_experts = w_gate.shape[0]
    logits = jnp.dot(normed, router, preferred_element_type=jnp.float32)
    chosen_mask = expert_ids[:, :, None] == jnp.arange(experts, dtype=jnp.int32)[None, None, :]
    chosen = jnp.sum(jnp.where(chosen_mask, logits[:, None, :], 0.0), axis=2)
    first_gate = jax.nn.sigmoid(chosen[:, 0] - chosen[:, 1])
    gates = jnp.stack([first_gate, 1.0 - first_gate], axis=1)
    pair_expert = expert_ids.reshape(row_count * top_count)
    pair_hot = chosen_mask.reshape(row_count * top_count, experts).astype(jnp.int32)
    pair_slot = jnp.sum((jnp.cumsum(pair_hot, axis=0) - 1) * pair_hot, axis=1)
    pair_rows = jnp.repeat(normed, top_count, axis=0)
    blocks = (
        jnp.zeros((experts, capacity, width), jnp.bfloat16)
        .at[pair_expert, pair_slot]
        .set(pair_rows)
    )
    blocks = blocks.reshape(members, local_experts, capacity, width)
    received = lax.all_to_all(blocks, "ep", split_axis=0, concat_axis=0, tiled=True)
    gate_part = jnp.einsum("pecd,edf->pecf", received, w_gate, preferred_element_type=jnp.float32)
    up_part = jnp.einsum("pecd,edf->pecf", received, w_up, preferred_element_type=jnp.float32)
    activated = (jax.nn.silu(gate_part) * up_part).astype(jnp.bfloat16)
    outputs = jnp.einsum(
        "pecf,efd->pecd", activated, w_down, preferred_element_type=jnp.float32
    ).astype(jnp.bfloat16)
    returned = lax.all_to_all(outputs, "ep", split_axis=0, concat_axis=0, tiled=True)
    returned = returned.reshape(experts, capacity, width)
    combined = returned[pair_expert, pair_slot].reshape(row_count, top_count, width)
    total = wide + jnp.sum(gates[:, :, None] * combined.astype(jnp.float32), axis=1)
    return total.astype(jnp.bfloat16)


def solution(mesh):
    placed = (
        P(("grp", "ep"), None),
        P(("grp", "ep")),
        P(("grp", "ep"), None),
        P("ep", None),
        P(),
        P("ep", None),
        P(),
        P(),
        P(),
        P("ep", None, None),
        P("ep", None, None),
        P("ep", None, None),
    )
    return jax.shard_map(
        shards, mesh=mesh, in_specs=placed, out_specs=P(("grp", "ep"), None), check_vma=False
    )
```

profile of v0, /device:TPU:0, one launch (start us, length us, event | category | flops | bytes accessed | tf_op | source)
XLA Modules:
  0.0 753.2 jit_solution(13190047248608267725)
XLA Ops:
  7.4 22.7 %all-gather = s32[8,1,256]{2,1,0:T(1,128)S(1)} all-gather(s32[1,1,256]{2,1,0:T(1,128)} %bitcast.118), channel_id=1, replica_groups=mesh['grp'=4,'ep'=8] {'ep'}, dimensions={0}, use_global_device_ids=true | all-gather | bytes 9216 | tf_op jit(solution)/shard_map/all_gather | solution.py:37
  31.9 3.8 sort.42
  35.7 2.1 gather_fusion
  37.8 3.6 all-to-all-start
  44.3 3.2 sort.44
  47.5 23.2 %all-to-all-done = bf16[8,32,1152]{2,1,0:T(8,128)(2,1)S(1)} async-done(((bf16[8,32,1152]{2,1,0:T(8,128)(2,1)}), bf16[8,32,1152]{2,1,0:T(8,128)(2,1)S(1)}, u32[]{:S(2)}, u32[]{:S(2)}) %all-to-all-start) | async-done | bytes 589856 | tf_op jit(solution)/shard_map/all_to_all | solution.py:42
  70.7 2.1 gather_fusion.1
  72.7 62.5 %all-gather.4.cloned.1.call-done = bf16[1152,2560]{1,0:T(8,128)(2,1)} async-done(((bf16[144,2560]{1,0:T(8,128)(2,1)}), bf16[1152,2560]{1,0:T(8,128)(2,1)}) %all-gather.4.cloned.1.call-update) | async-done | bytes 5898256 | tf_op jit(solution)/shard_map/all_gather | solution.py:10
  135.3 182.6 %all-gather.6.cloned.1.call-done = bf16[2560,2560]{1,0:T(8,128)(2,1)} async-done(((bf16[320,2560]{1,0:T(8,128)(2,1)}), bf16[2560,2560]{1,0:T(8,128)(2,1)}) %all-gather.6.cloned.1.call-update) | async-done | bytes 13107216 | tf_op jit(solution)/shard_map/all_gather | solution.py:13
  317.9 18.2 %fusion.9 = (f32[256]{0:T(256)S(1)}, bf16[256,2560]{1,0:T(8,128)(2,1)}) fusion(f32[2560]{0:T(1024)S(1)} %copy-done.8, bf16[2560,2560]{1,0:T(8,128)(2,1)} %all-gather.6.cloned.1.call-done, bf16[256,1152]{1,0:T(8,128)(2,1)} %gather_fusion.1, bf16[1152,2560]{1,0:T(8,128)(2,1)} %all-gather.4.cloned.1.call-done, f32[2560]{0:T(1024)S(1)} %copy-done.9), kind=kOutput, calls=%fused_computation.21 | convolution fusion | flops 4911923200 | bytes 20927488 | tf_op jit(solution)/shard_map/dot_general | solution.py:14
  338.9 3.0 broadcast_in_dim.43
  342.0 6.7 reshape.153
  348.6 2.8 broadcast_in_dim.42
  351.4 103.1 %scatter_fusion = bf16[8,128,2560]{2,1,0:T(8,128)(2,1)} fusion(bf16[8,128,2560]{2,1,0:T(8,128)(2,1)} %broadcast_in_dim.42, s32[512]{0:T(512)S(1)} %bitcast.115, bf16[512,2560]{1,0:T(8,128)(2,1)} %reshape.153), kind=kCustom, calls=%fused_computation.3 | custom fusion | bytes 7868416 | tf_op jit(solution)/shard_map/scatter | solution.py:64
  454.5 119.1 %all_to_all.22 = bf16[8,1,128,2560]{3,2,1,0:T(8,128)(2,1)S(1)} all-to-all(bf16[8,1,128,2560]{3,2,1,0:T(8,128)(2,1)} %bitcast.112), channel_id=1, replica_groups=mesh['grp'=4,'ep'=8] {'ep'}, dimensions={0} | all-to-all | bytes 10485760 | tf_op jit(solution)/shard_map/all_to_all | solution.py:67
  573.6 2.3 copy-done.3
  575.9 4.2 fusion.2
  580.1 10.3 %fusion.4 = bf16[8,1,128,2560]{3,2,1,0:T(8,128)(2,1)} fusion(bf16[1,512,2560]{2,1,0:T(8,128)(2,1)S(1)} %copy-done, bf16[1,2560,512]{2,1,0:T(8,128)(2,1)} %param.22, bf16[8,1,128,2560]{3,2,1,0:T(8,128)(2,1)} %copy-done.3, f32[8,128,512]{2,1,0:T(8,128)} %fusion.2), kind=kOutput, calls=%fused_computation.10 | convolution fusion | flops 5374476288 | bytes 17825792 | tf_op jit(solution)/shard_map/pecf,efd->pecd/dot_general | solution.py:71
  590.4 5.0 all-to-all-start.2
  597.4 112.4 %all-to-all-done.2 = bf16[8,1,128,2560]{3,2,1,0:T(8,128)(2,1)} async-done(((bf16[8,1,128,2560]{3,2,1,0:T(8,128)(2,1)}), bf16[8,1,128,2560]{3,2,1,0:T(8,128)(2,1)}, u32[]{:S(2)}, u32[]{:S(2)}) %all-to-all-start.2) | async-done | bytes 5242912 | tf_op jit(solution)/shard_map/all_to_all | solution.py:74
  709.9 14.0 %gather_fusion.2 = bf16[512,2560]{1,0:T(8,128)(2,1)} fusion(bf16[8,128,2560]{2,1,0:T(8,128)(2,1)} %bitcast.28, s32[512]{0:T(512)S(1)} %bitcast.114), kind=kCustom, calls=%fused_computation.2 | custom fusion | bytes 5246976 | tf_op jit(solution)/shard_map/gather | solution.py:76
  723.8 7.0 reshape.128
  730.8 11.6 %multiply_reduce_fusion = f32[256,2560]{1,0:T(8,128)} fusion(f32[256,2,2560]{2,1,0:T(2,128)} %reshape.128, f32[256,2]{1,0:T(8,128)S(1)} %copy.27), kind=kLoop, calls=%fused_computation.9 | loop fusion | flops 1966080 | bytes 7866368 | tf_op jit(solution)/shard_map/reduce_sum | solution.py:77
  742.4 3.5 fusion.12
  (53 shorter events, 9.4 us)
Async XLA Ops:
  7.4 572.7 %copy-start = (bf16[1,512,2560]{2,1,0:T(8,128)(2,1)S(1)}, bf16[1,512,2560]{2,1,0:T(8,128)(2,1)}, u32[]{:S(2)}) copy-start(bf16[1,512,2560]{2,1,0:T(8,128)(2,1)} %param.23) | copy-start | bytes 7864324
  7.4 28.3 %copy-start.1 = (bf16[256,1152]{1,0:T(8,128)(2,1)S(1)}, bf16[256,1152]{1,0:T(8,128)(2,1)}, u32[]{:S(2)}) copy-start(bf16[256,1152]{1,0:T(8,128)(2,1)} %param.12) | copy-start | bytes 1769476
  7.4 36.1 %sort.46.cloned.1.call-start = ((), (), s32[]{:S(2)}) async-start(), calls=%async_computation.5 | async-start | bytes 24608 | tf_op jit(solution)/shard_map/jit(sort)/sort | solution.py:40
  30.7 104.6 %all-gather.4.cloned.1.call-start = ((), (), s32[]{:S(2)}) async-start(), calls=%async_computation.3 | async-start | bytes 6635520 | tf_op jit(solution)/shard_map/all_gather | solution.py:10
  31.3 286.6 %all-gather.6.cloned.1.call-start = ((), (), s32[]{:S(2)}) async-start(), calls=%async_computation.4 | async-start | bytes 14745600 | tf_op jit(solution)/shard_map/all_gather | solution.py:13
  35.7 5.6 copy-start.6
  37.8 32.9 %all-to-all-start = ((bf16[8,32,1152]{2,1,0:T(8,128)(2,1)}), bf16[8,32,1152]{2,1,0:T(8,128)(2,1)S(1)}, u32[]{:S(2)}, u32[]{:S(2)}) async-start(bf16[8,32,1152]{2,1,0:T(8,128)(2,1)} %bitcast.116), calls=%async_computation | async-start | bytes 1179648 | tf_op jit(solution)/shard_map/all_to_all | solution.py:42
  70.7 247.2 %copy-start.8 = (f32[2560]{0:T(1024)S(1)}, f32[2560]{0:T(1024)}, u32[]{:S(2)}) copy-start(f32[2560]{0:T(1024)} %param.18) | copy-start | bytes 30724
  70.7 247.2 %copy-start.9 = (f32[2560]{0:T(1024)S(1)}, f32[2560]{0:T(1024)}, u32[]{:S(2)}) copy-start(f32[2560]{0:T(1024)} %param.16) | copy-start | bytes 30724
  72.7 263.4 %copy-start.5 = (f32[2560]{0:T(1024)S(1)}, f32[2560]{0:T(1024)}, u32[]{:S(2)}) copy-start(f32[2560]{0:T(1024)} %param.19) | copy-start | bytes 30724
  337.8 1.1 copy-start.2
  454.5 121.5 %copy-start.7 = (bf16[1,2560,512]{2,1,0:T(8,128)(2,1)S(1)}, bf16[1,2560,512]{2,1,0:T(8,128)(2,1)}, u32[]{:S(2)}) copy-start(bf16[1,2560,512]{2,1,0:T(8,128)(2,1)} %param.21) | copy-start | bytes 7864324
  573.6 2.3 copy-start.3
  590.4 5.0 copy-start.4
  590.4 119.4 %all-to-all-start.2 = ((bf16[8,1,128,2560]{3,2,1,0:T(8,128)(2,1)}), bf16[8,1,128,2560]{3,2,1,0:T(8,128)(2,1)}, u32[]{:S(2)}, u32[]{:S(2)}) async-start(bf16[8,1,128,2560]{3,2,1,0:T(8,128)(2,1)} %fusion.4), calls=%async_computation.2 | async-start | bytes 10485760 | tf_op jit(solution)/shard_map/all_to_all | solution.py:74
Sparse Core Ops, SparseCore 0:
  30.8 2.3 sort.48.cloned.1.call-done
  (1 shorter events, 0.0 us)
Sparse Core Ops, SparseCore 1:
  33.4 101.9 all-gather.3
  137.4 180.5 all-gather.5
where the time goes:
time: 756 us; the launch traced here: 753 us
  waiting for transfers between devices  382 us (51%)
  local copies, waits for them, and re-layouts  146 us (19%)
  blocking collectives  142 us (19%)
  matrix products  34.4 us (5%)
  other arithmetic  25.7 us (3%)
  between operations  15 us (2%)
  starting transfers between devices  8.65 us (1%)
    all_gather x1, waiting for transfers between devices, project(): second_full = lax.all_gather(proj_out, 'ep', axis=0, tiled=True)  183 us
    all_to_all x1, blocking collectives, shards(): lax.all_to_all(blocks, 'ep', split_axis=0, concat_axis=0, tiled=True)  119 us
    all_to_all x1, waiting for transfers between devices, shards(): lax.all_to_all(outputs, 'ep', split_axis=0, concat_axis=0, tiled=True)  112 us
    scatter x1, local copies, waits for them, and re-layouts, shards(): blocks = jnp.zeros((experts, capacity, width), jnp.bfloat16).at[pair_expe...  103 us
    all_gather x1, waiting for transfers between devices, project(): first_full = lax.all_gather(proj_in, 'ep', axis=0, tiled=True)  62.5 us
    all_to_all x1, waiting for transfers between devices, shards(): lax.all_to_all(features[sender_order], 'ep', split_axis=0, concat_axis=0,...  23.2 us
    all_gather x1, blocking collectives, shards(): lax.all_gather(token_position, 'ep', axis=0, tiled=True)  22.7 us
    dot_general x1, matrix products, project(): result = jnp.dot(hidden, second_full, preferred_element_type=jnp.float32)  18.2 us
  transfers between devices with their start and end apart: 4, of which 4 were waited for; matrix products, arithmetic and copies ran while one was open for 2% of the time, Pallas kernels for 0%

commit v1 on v0

v1 whole, which is shorter than its diff:
```python
import jax
import jax.numpy as jnp
from jax import lax
from jax.sharding import PartitionSpec as P

EPSILON = 1e-06
F32 = jnp.float32
BF16 = jnp.bfloat16


def select_rows(mask, rows):
    return jnp.dot(mask.astype(BF16), rows, preferred_element_type=F32).astype(BF16)


def gather_columns(weight):
    members = lax.axis_size("grp")
    width = weight.shape[1] // members
    part = lax.dynamic_slice_in_dim(weight, lax.axis_index("grp") * width, width, 1)
    full = lax.all_gather(part, ("grp", "ep"), axis=0, tiled=True)
    return full.reshape(members, -1, width)


def shards(
    features,
    token_position,
    expert_ids,
    proj_in,
    bias_in,
    proj_out,
    bias_out,
    norm_gain,
    router,
    w_gate,
    w_up,
    w_down,
):
    members = lax.axis_size("ep")
    row_count, vis = features.shape
    width = proj_in.shape[1]
    first_full = gather_columns(proj_in)
    second_full = gather_columns(proj_out)

    index = jnp.arange(row_count, dtype=jnp.int32)
    rank = jnp.sum((token_position[None, :] < token_position[:, None]).astype(jnp.int32), axis=1)
    local = token_position % row_count
    lane = jnp.arange(128, dtype=jnp.int32)[None, :]
    high, low = (local // 16)[:, None], (local % 16)[:, None]
    tail = jnp.where(lane == 0, high, jnp.where(lane == 1, low, 0)).astype(BF16)
    order = rank[None, :] == index[:, None]
    sent = select_rows(order, jnp.concatenate([features, tail], axis=1))
    arrived = lax.all_to_all(sent, "ep", split_axis=0, concat_axis=0, tiled=True)
    landing = (arrived[:, vis].astype(F32) * 16 + arrived[:, vis + 1].astype(F32)).astype(jnp.int32)
    patches = select_rows(landing[None, :] == index[:, None], arrived[:, :vis])

    pre_act = jnp.einsum("rk,gkn->rgn", patches, first_full, preferred_element_type=F32)
    pre_act = pre_act.reshape(row_count, width)
    hidden = jax.nn.gelu(pre_act + bias_in, approximate=False).astype(BF16)
    result = jnp.einsum("rk,gkn->rgn", hidden, second_full, preferred_element_type=F32)
    tokens = (result.reshape(row_count, width) + bias_out).astype(BF16)

    wide = tokens.astype(F32)
    scale = lax.rsqrt(jnp.mean(wide * wide, axis=-1, keepdims=True) + EPSILON)
    normed = (wide * scale * norm_gain).astype(BF16)
    experts = router.shape[1]
    top_count = expert_ids.shape[1]
    capacity = 2 * row_count * top_count // experts
    local_experts = w_gate.shape[0]
    logits = jnp.dot(normed, router, preferred_element_type=F32)
    numbers = jnp.arange(experts, dtype=jnp.int32)
    chosen_mask = expert_ids[:, :, None] == numbers[None, None, :]
    chosen = jnp.sum(jnp.where(chosen_mask, logits[:, None, :], 0.0), axis=2)
    first_gate = jax.nn.sigmoid(chosen[:, 0] - chosen[:, 1])
    gates = (first_gate, 1.0 - first_gate)

    named = jnp.any(chosen_mask, axis=1)
    earlier = (index[None, :] < index[:, None]).astype(BF16)
    before = jnp.dot(earlier, named.astype(BF16), preferred_element_type=F32).astype(jnp.int32)
    place = jnp.where(named, before, -1)
    slots = jnp.arange(capacity, dtype=jnp.int32)
    filled = place.T[:, None, :] == slots[None, :, None]
    blocks = select_rows(filled.reshape(experts * capacity, row_count), normed)
    blocks = blocks.reshape(members, local_experts, capacity, width)
    received = lax.all_to_all(blocks, "ep", split_axis=0, concat_axis=0, tiled=True)
    gate_part = jnp.einsum("pecd,edf->pecf", received, w_gate, preferred_element_type=F32)
    up_part = jnp.einsum("pecd,edf->pecf", received, w_up, preferred_element_type=F32)
    activated = (jax.nn.silu(gate_part) * up_part).astype(BF16)
    outputs = jnp.einsum("pecf,efd->pecd", activated, w_down, preferred_element_type=F32).astype(BF16)
    returned = lax.all_to_all(outputs, "ep", split_axis=0, concat_axis=0, tiled=True)
    returned = returned.reshape(experts * capacity, width)
    total = 0.0
    for choice in range(top_count):
        slot = jnp.where(chosen_mask[:, choice], before, -1)
        picked = (slot[:, :, None] == slots[None, None, :]).reshape(row_count, experts * capacity)
        row = jnp.dot(picked.astype(BF16), returned, preferred_element_type=F32)
        total = total + gates[choice][:, None] * row
    return (wide + total).astype(BF16)


def solution(mesh):
    placed = (
        P(("grp", "ep"), None),
        P(("grp", "ep")),
        P(("grp", "ep"), None),
        P("ep", None),
        P(),
        P("ep", None),
        P(),
        P(),
        P(),
        P("ep", None, None),
        P("ep", None, None),
        P("ep", None, None),
    )
    return jax.shard_map(
        shards, mesh=mesh, in_specs=placed, out_specs=P(("grp", "ep"), None), check_vma=False
    )
```

time: 756 us -> 496 us (0.66)
  waiting for transfers between devices: 382 us -> 261 us
  local copies, waits for them, and re-layouts: 146 us -> 35.4 us
  other arithmetic: 25.7 us -> 2.74 us
  blocking collectives: 142 us -> 120 us
  matrix products: 34.4 us -> 48.7 us
    all_gather x2, waiting for transfers between devices: 245 us -> 129 us  [gather_columns(): full = lax.all_gather(part, ('grp', 'ep'), axis=0, tiled=True)]
    scatter x1 -> x0, local copies, waits for them, and re-layouts: 103 us -> none  [shards(): blocks = jnp.zeros((experts, capacity, width), jnp.bfloat16).at[pair_expe...]
    dot_general x0 -> x2, local copies, waits for them, and re-layouts: none -> 26.6 us  [the longest x1 17.7 us: shards(): jnp.einsum('rk,gkn->rgn', hidden, second_full, preferred_element_type=F32)]
    all_gather x1 -> x0, blocking collectives: 22.7 us -> none  [shards(): lax.all_gather(token_position, 'ep', axis=0, tiled=True)]
    gather x3 -> x0, local copies, waits for them, and re-layouts: 18.1 us -> none  [the longest x1 14 us: shards(): returned[pair_expert, pair_slot].reshape(row_count, top_count, width)]
    dot_general x4 -> x10, matrix products: 34.4 us -> 48.7 us  [the longest x1 15.8 us: shards(): jnp.einsum('rk,gkn->rgn', hidden, second_full, preferred_element_type=F32)]
    reduce_sum x2 -> x1, other arithmetic: 11.6 us -> 0.93 us  [shards(): jnp.sum((token_position[None, :] < token_position[:, None]).astype(jnp.in...]
  transfers between devices with their start and end apart: 4 -> 4, of which waited for: 4 -> 4; matrix products, arithmetic and copies ran while one was open for 2% -> 5% of each run, Pallas kernels for 0% -> 0%
where the time goes in v1:
time: 496 us; the launch traced here: 494 us
  waiting for transfers between devices  261 us (53%)
  blocking collectives  120 us (24%)
  matrix products  48.7 us (10%)
  local copies, waits for them, and re-layouts  35.4 us (7%)
  between operations  13.6 us (3%)
  starting transfers between devices  12.2 us (2%)
    all_gather x2, waiting for transfers between devices, gather_columns(): full = lax.all_gather(part, ('grp', 'ep'), axis=0, tiled=True)  129 us
    all_to_all x1, blocking collectives, shards(): lax.all_to_all(blocks, 'ep', split_axis=0, concat_axis=0, tiled=True)  120 us
    all_to_all x1, waiting for transfers between devices, shards(): lax.all_to_all(outputs, 'ep', split_axis=0, concat_axis=0, tiled=True)  112 us
    all_to_all x1, waiting for transfers between devices, shards(): lax.all_to_all(sent, 'ep', split_axis=0, concat_axis=0, tiled=True)  20.2 us
    dot_general x1, local copies, waits for them, and re-layouts, shards(): jnp.einsum('rk,gkn->rgn', hidden, second_full, preferred_element_type=F32)  17.7 us
    dot_general x1, matrix products, shards(): jnp.einsum('rk,gkn->rgn', hidden, second_full, preferred_element_type=F32)  15.8 us
    dot_general x1, matrix products, shards(): jnp.einsum('pecf,efd->pecd', activated, w_down, preferred_element_type=F32)  10.3 us
  transfers between devices with their start and end apart: 4, of which 4 were waited for; matrix products, arithmetic and copies ran while one was open for 5% of the time, Pallas kernels for 0%

profile of v1, /device:TPU:0, one launch (start us, length us, event | category | flops | bytes accessed | tf_op | source)
XLA Modules:
  0.0 494.2 jit_solution(15530253404360054965)
XLA Ops:
  6.5 1.8 constant_dynamic-slice_fusion.1
  8.4 1.8 constant_dynamic-slice_fusion
  10.2 0.9 convert_reduce_fusion
  12.0 2.2 convolution_convert_fusion.3
  14.3 7.3 %all-to-all-start = ((bf16[8,32,1280]{2,1,0:T(8,128)(2,1)}), bf16[8,32,1280]{2,1,0:T(8,128)(2,1)S(1)}, u32[]{:S(2)}, u32[]{:S(2)}) async-start(bf16[8,32,1280]{2,1,0:T(8,128)(2,1)} %bitcast.128), calls=%async_computation | async-start | bytes 1310720 | tf_op jit(solution)/shard_map/all_to_all | solution.py:51
  22.6 20.2 %all-to-all-done = bf16[8,32,1280]{2,1,0:T(8,128)(2,1)S(1)} async-done(((bf16[8,32,1280]{2,1,0:T(8,128)(2,1)}), bf16[8,32,1280]{2,1,0:T(8,128)(2,1)S(1)}, u32[]{:S(2)}, u32[]{:S(2)}) %all-to-all-start) | async-done | bytes 655392 | tf_op jit(solution)/shard_map/all_to_all | solution.py:51
  43.5 0.9 copy.43
  44.5 0.9 copy.42
  45.4 1.2 convolution_convert_fusion.2
  46.6 38.9 %all-gather.3.cloned.1.call-done = bf16[4608,640]{1,0:T(8,128)(2,1)} async-done(((bf16[144,640]{1,0:T(8,128)(2,1)}), bf16[4608,640]{1,0:T(8,128)(2,1)}) %all-gather.3.cloned.1.call-update) | async-done | bytes 5898256 | tf_op jit(solution)/shard_map/all_gather | solution.py:19
  85.4 8.9 %copy.36 = bf16[4,640,1152]{2,1,0:T(8,128)(2,1)} copy(bf16[4,640,1152]{1,2,0:T(8,128)(2,1)} %bitcast.124) | data formatting | bytes 11796480 | tf_op jit(solution)/shard_map/rk,gkn->rgn/dot_general | solution.py:55
  94.3 90.3 %all-gather.5.cloned.1.call-done = bf16[10240,640]{1,0:T(8,128)(2,1)} async-done(((bf16[320,640]{1,0:T(8,128)(2,1)}), bf16[10240,640]{1,0:T(8,128)(2,1)}) %all-gather.5.cloned.1.call-update) | async-done | bytes 13107216 | tf_op jit(solution)/shard_map/all_gather | solution.py:19
  184.7 17.7 %copy.37 = bf16[4,640,2560]{2,1,0:T(8,128)(2,1)} copy(bf16[4,640,2560]{1,2,0:T(8,128)(2,1)} %bitcast.122) | data formatting | bytes 26214400 | tf_op jit(solution)/shard_map/rk,gkn->rgn/dot_general | solution.py:58
  202.4 15.8 %fusion.12 = (f32[256]{0:T(256)S(1)}, bf16[256,2560]{1,0:T(8,128)(2,1)}) fusion(f32[2560]{0:T(1024)S(1)} %copy-done.12, bf16[2560,2560]{1,0:T(8,128)(2,1)} %bitcast.123, bf16[256,1152]{1,0:T(8,128)(2,1)S(1)} %copy-done.3, bf16[2560,1152]{1,0:T(8,128)(2,1)} %bitcast.125, f32[2560]{0:T(1024)S(1)} %copy-done.13), kind=kOutput, calls=%fused_computation.21 | convolution fusion | flops 4911923200 | bytes 20927488 | tf_op jit(solution)/shard_map/rk,gkn->rgn/dot_general | solution.py:58
  218.3 3.0 convolution_convert_fusion
  221.2 120.1 %all_to_all.22 = bf16[8,1,128,2560]{3,2,1,0:T(8,128)(2,1)S(1)} all-to-all(bf16[8,1,128,2560]{3,2,1,0:T(8,128)(2,1)S(1)} %bitcast.121), channel_id=1, replica_groups=mesh['grp'=4,'ep'=8] {'ep'}, dimensions={0} | all-to-all | bytes 10485760 | tf_op jit(solution)/shard_map/all_to_all | solution.py:83
  341.4 2.4 copy-done.1
  343.7 4.2 fusion.2
  347.9 10.3 %fusion.4 = bf16[8,1,128,2560]{3,2,1,0:T(8,128)(2,1)} fusion(bf16[1,512,2560]{2,1,0:T(8,128)(2,1)S(1)} %copy-done, bf16[1,2560,512]{2,1,0:T(8,128)(2,1)} %param.22, bf16[8,1,128,2560]{3,2,1,0:T(8,128)(2,1)} %copy-done.1, f32[8,128,512]{2,1,0:T(8,128)} %fusion.2), kind=kOutput, calls=%fused_computation.6 | convolution fusion | flops 5374476288 | bytes 17825792 | tf_op jit(solution)/shard_map/pecf,efd->pecd/dot_general | solution.py:87
  358.3 4.8 all-to-all-start.2
  364.1 1.8 fusion.82
  366.0 112.0 %all-to-all-done.2 = bf16[8,1,128,2560]{3,2,1,0:T(8,128)(2,1)} async-done(((bf16[8,1,128,2560]{3,2,1,0:T(8,128)(2,1)}), bf16[8,1,128,2560]{3,2,1,0:T(8,128)(2,1)}, u32[]{:S(2)}, u32[]{:S(2)}) %all-to-all-start.2) | async-done | bytes 5242912 | tf_op jit(solution)/shard_map/all_to_all | solution.py:88
  478.0 4.1 convolution_multiply_fusion
  482.1 5.2 %fusion.7 = bf16[256,2560]{1,0:T(8,128)(2,1)} fusion(f32[256,2560]{1,0:T(8,128)S(1)} %convolution_multiply_fusion, bf16[1024,2560]{1,0:T(8,128)(2,1)} %bitcast.36, bf16[256,2560]{1,0:T(8,128)(2,1)S(1)} %copy-done.2, f32[256]{0:T(256)S(1)} %bitcast.132, pred[32,8,8,128]{3,2,1,0:T(8,128)(4,1)S(1)} %bitcast.129), kind=kOutput, calls=%fused_computation.16 | convolution fusion | flops 1345454080 | bytes 10748928 | tf_op jit(solution)/shard_map/dot_general | solution.py:94
  (48 shorter events, 3.7 us)
Async XLA Ops:
  6.5 341.4 %copy-start = (bf16[1,512,2560]{2,1,0:T(8,128)(2,1)S(1)}, bf16[1,512,2560]{2,1,0:T(8,128)(2,1)}, u32[]{:S(2)}) copy-start(bf16[1,512,2560]{2,1,0:T(8,128)(2,1)} %param.23) | copy-start | bytes 7864324
  6.5 15.0 %copy-start.7 = (s32[256,2]{0,1:T(2,128)S(1)}, s32[256,2]{0,1:T(2,128)}, u32[]{:S(2)}) copy-start(s32[256,2]{0,1:T(2,128)} %param.14) | copy-start | bytes 6148
  6.5 78.9 %all-gather.3.cloned.1.call-start = ((), (), s32[]{:S(2)}) async-start(), calls=%async_computation.3 | async-start | bytes 6082560 | tf_op jit(solution)/shard_map/all_gather | solution.py:19
  8.4 176.3 %all-gather.5.cloned.1.call-start = ((), (), s32[]{:S(2)}) async-start(), calls=%async_computation.4 | async-start | bytes 13516800 | tf_op jit(solution)/shard_map/all_gather | solution.py:19
  14.3 28.6 %all-to-all-start = ((bf16[8,32,1280]{2,1,0:T(8,128)(2,1)}), bf16[8,32,1280]{2,1,0:T(8,128)(2,1)S(1)}, u32[]{:S(2)}, u32[]{:S(2)}) async-start(bf16[8,32,1280]{2,1,0:T(8,128)(2,1)} %bitcast.128), calls=%async_computation | async-start | bytes 1310720 | tf_op jit(solution)/shard_map/all_to_all | solution.py:51
  184.7 17.7 %copy-start.3 = (bf16[256,1152]{1,0:T(8,128)(2,1)S(1)}, bf16[256,1152]{1,0:T(8,128)(2,1)}, u32[]{:S(2)}) copy-start(bf16[256,1152]{1,0:T(8,128)(2,1)} %convolution_convert_fusion.2) | copy-start | bytes 1769476
  184.7 17.7 %copy-start.12 = (f32[2560]{0:T(1024)S(1)}, f32[2560]{0:T(1024)}, u32[]{:S(2)}) copy-start(f32[2560]{0:T(1024)} %param.18) | copy-start | bytes 30724
  184.7 17.7 %copy-start.13 = (f32[2560]{0:T(1024)S(1)}, f32[2560]{0:T(1024)}, u32[]{:S(2)}) copy-start(f32[2560]{0:T(1024)} %param.16) | copy-start | bytes 30724
  202.4 15.9 %copy-start.4 = (f32[2560]{0:T(1024)S(1)}, f32[2560]{0:T(1024)}, u32[]{:S(2)}) copy-start(f32[2560]{0:T(1024)} %param.19) | copy-start | bytes 30724
  218.2 3.0 copy-start.8
  221.2 122.5 %copy-start.10 = (bf16[1,2560,512]{2,1,0:T(8,128)(2,1)S(1)}, bf16[1,2560,512]{2,1,0:T(8,128)(2,1)}, u32[]{:S(2)}) copy-start(bf16[1,2560,512]{2,1,0:T(8,128)(2,1)} %param.21) | copy-start | bytes 7864324
  341.4 2.4 copy-start.1
  358.3 4.8 copy-start.6
  358.3 5.0 %copy-start.5 = (s32[256,8]{0,1:T(8,128)S(1)}, s32[256,8]{0,1:T(8,128)}, u32[]{:S(2)}) copy-start(s32[256,8]{0,1:T(8,128)} %get-tuple-element.11) | copy-start | bytes 24580
  358.3 5.8 %copy-start.9 = (f32[256]{0:T(256)S(1)}, f32[256]{0:T(256)}, u32[]{:S(2)}) copy-start(f32[256]{0:T(256)} %copy-done.8) | copy-start | bytes 3076
  358.3 5.8 %copy-start.11 = (bf16[2560,8]{0,1:T(8,128)(2,1)S(1)}, bf16[2560,8]{0,1:T(8,128)(2,1)}, u32[]{:S(2)}) copy-start(bf16[2560,8]{0,1:T(8,128)(2,1)} %param.20) | copy-start | bytes 122884
  358.3 119.7 %all-to-all-start.2 = ((bf16[8,1,128,2560]{3,2,1,0:T(8,128)(2,1)}), bf16[8,1,128,2560]{3,2,1,0:T(8,128)(2,1)}, u32[]{:S(2)}, u32[]{:S(2)}) async-start(bf16[8,1,128,2560]{3,2,1,0:T(8,128)(2,1)} %fusion.4), calls=%async_computation.2 | async-start | bytes 10485760 | tf_op jit(solution)/shard_map/all_to_all | solution.py:88
  478.0 4.1 copy-start.2
Sparse Core Ops, SparseCore 0:
  10.2 75.1 all-gather.2
  88.3 96.3 all-gather.4

commit v2 on v1

v2 whole, which is shorter than its diff:
```python
import jax
import jax.numpy as jnp
from jax import lax
from jax.sharding import PartitionSpec as P

EPSILON = 1e-06
F32 = jnp.float32
BF16 = jnp.bfloat16
CHUNKS = 2


def select_rows(mask, rows):
    return jnp.dot(mask.astype(BF16), rows, preferred_element_type=F32).astype(BF16)


def gather_columns(weight):
    members = lax.axis_size("grp")
    width = weight.shape[1] // members
    part = lax.dynamic_slice_in_dim(weight, lax.axis_index("grp") * width, width, 1)
    full = lax.all_gather(part, ("grp", "ep"), axis=0, tiled=True)
    return full.reshape(members, -1, width)


def gather_rows(weight, column, width):
    depth = weight.shape[0] // lax.axis_size("grp")
    start = lax.axis_index("grp") * depth
    part = lax.dynamic_slice(weight, (start, column), (depth, width))
    return lax.all_gather(part, ("ep", "grp"), axis=0, tiled=True)


def shards(
    features,
    token_position,
    expert_ids,
    proj_in,
    bias_in,
    proj_out,
    bias_out,
    norm_gain,
    router,
    w_gate,
    w_up,
    w_down,
):
    members = lax.axis_size("ep")
    row_count, vis = features.shape
    width = proj_in.shape[1]
    step = width // CHUNKS
    columns = [slice(c * step, (c + 1) * step) for c in range(CHUNKS)]
    first_full = gather_columns(proj_in)
    second_full = [gather_rows(proj_out, c * step, step) for c in range(CHUNKS)]

    index = jnp.arange(row_count, dtype=jnp.int32)
    rank = jnp.sum((token_position[None, :] < token_position[:, None]).astype(jnp.int32), axis=1)
    local = token_position % row_count
    lane = jnp.arange(128, dtype=jnp.int32)[None, :]
    high, low = (local // 16)[:, None], (local % 16)[:, None]
    tail = jnp.where(lane == 0, high, jnp.where(lane == 1, low, 0)).astype(BF16)
    order = rank[None, :] == index[:, None]
    sent = select_rows(order, jnp.concatenate([features, tail], axis=1))
    arrived = lax.all_to_all(sent, "ep", split_axis=0, concat_axis=0, tiled=True)
    landing = (arrived[:, vis].astype(F32) * 16 + arrived[:, vis + 1].astype(F32)).astype(jnp.int32)
    patches = select_rows(landing[None, :] == index[:, None], arrived[:, :vis])

    parts = first_full.shape[0]
    pieces = []
    for g, bias in enumerate(jnp.split(bias_in, parts)):
        pre_act = jnp.dot(patches, first_full[g], preferred_element_type=F32)
        pieces.append(jax.nn.gelu(pre_act + bias, approximate=False).astype(BF16))
    hidden = jnp.concatenate(pieces, axis=1)

    experts = router.shape[1]
    top_count = expert_ids.shape[1]
    capacity = 2 * row_count * top_count // experts
    local_experts = w_gate.shape[0]
    numbers = jnp.arange(experts, dtype=jnp.int32)
    chosen_mask = expert_ids[:, :, None] == numbers[None, None, :]
    named = jnp.any(chosen_mask, axis=1)
    earlier = (index[None, :] < index[:, None]).astype(BF16)
    before = jnp.dot(earlier, named.astype(BF16), preferred_element_type=F32).astype(jnp.int32)
    place = jnp.where(named, before, -1)
    slots = jnp.arange(capacity, dtype=jnp.int32)
    filled = (place.T[:, None, :] == slots[None, :, None]).reshape(experts * capacity, row_count)
    filled = filled.astype(BF16)

    tokens, received = [], []
    for c, cols in enumerate(columns):
        result = jnp.dot(hidden, second_full[c], preferred_element_type=F32)
        part = (result + bias_out[cols]).astype(BF16)
        blocks = select_rows(filled, part).reshape(members, local_experts, capacity, step)
        tokens.append(part)
        received.append(lax.all_to_all(blocks, "ep", split_axis=0, concat_axis=0, tiled=True))

    def normed_parts(parts):
        wide = [part.astype(F32) for part in parts]
        square = sum(jnp.sum(part * part, axis=-1, keepdims=True) for part in wide)
        scale = lax.rsqrt(square / width + EPSILON)
        return [(part * scale * norm_gain[cols]).astype(BF16) for part, cols in zip(wide, columns)]

    normed = normed_parts(tokens)
    logits = sum(
        jnp.dot(part, router[cols], preferred_element_type=F32)
        for part, cols in zip(normed, columns)
    )
    chosen = jnp.sum(jnp.where(chosen_mask, logits[:, None, :], 0.0), axis=2)
    first_gate = jax.nn.sigmoid(chosen[:, 0] - chosen[:, 1])
    gates = (first_gate, 1.0 - first_gate)

    def expand(rows, weight):
        return sum(
            jnp.einsum("pecd,edf->pecf", part, weight[:, cols], preferred_element_type=F32)
            for part, cols in zip(rows, columns)
        )

    rows = normed_parts(received)
    activated = (jax.nn.silu(expand(rows, w_gate)) * expand(rows, w_up)).astype(BF16)
    picked = []
    for choice in range(top_count):
        slot = jnp.where(chosen_mask[:, choice], before, -1)
        picked.append((slot[:, :, None] == slots[None, None, :]).reshape(row_count, experts * capacity))
    mixed = []
    for part, cols in zip(tokens, columns):
        outputs = jnp.einsum(
            "pecf,efd->pecd", activated, w_down[:, :, cols], preferred_element_type=F32
        ).astype(BF16)
        returned = lax.all_to_all(outputs, "ep", split_axis=0, concat_axis=0, tiled=True)
        returned = returned.reshape(experts * capacity, step)
        total = 0.0
        for choice in range(top_count):
            row = jnp.dot(picked[choice].astype(BF16), returned, preferred_element_type=F32)
            total = total + gates[choice][:, None] * row
        mixed.append((part.astype(F32) + total).astype(BF16))
    return jnp.concatenate(mixed, axis=1)


def solution(mesh):
    placed = (
        P(("grp", "ep"), None),
        P(("grp", "ep")),
        P(("grp", "ep"), None),
        P("ep", None),
        P(),
        P("ep", None),
        P(),
        P(),
        P(),
        P("ep", None, None),
        P("ep", None, None),
        P("ep", None, None),
    )
    return jax.shard_map(
        shards, mesh=mesh, in_specs=placed, out_specs=P(("grp", "ep"), None), check_vma=False
    )
```

time: 496 us -> 494 us (level)
  waiting for transfers between devices: 261 us -> 385 us
  blocking collectives: 120 us -> 0 us
  local copies, waits for them, and re-layouts: 35.4 us -> 6.9 us
  starting transfers between devices: 12.2 us -> 24.2 us
  matrix products: 48.7 us -> 55 us
  other arithmetic: 2.74 us -> 8.72 us
    all_gather x0 -> x2, waiting for transfers between devices: none -> 154 us  [gather_rows(): return lax.all_gather(part, ('ep', 'grp'), axis=0, tiled=True)]
    all_to_all x1 -> x0, blocking collectives: 120 us -> none  [shards(): lax.all_to_all(blocks, 'ep', split_axis=0, concat_axis=0, tiled=True)]
    all_gather x2 -> x1, waiting for transfers between devices: 129 us -> 42.8 us  [gather_columns(): full = lax.all_gather(part, ('grp', 'ep'), axis=0, tiled=True)]
    all_to_all x0 -> x2, waiting for transfers between devices: none -> 59.6 us  [shards(): lax.all_to_all(blocks, 'ep', split_axis=0, concat_axis=0, tiled=True)]
    dot_general x2 -> x0, local copies, waits for them, and re-layouts: 26.6 us -> none  [the longest x1 17.7 us: shards(): jnp.einsum('rk,gkn->rgn', hidden, second_full, preferred_element_type=F32)]
    all_to_all x0 -> x2, starting transfers between devices: none -> 8.54 us  [shards(): lax.all_to_all(blocks, 'ep', split_axis=0, concat_axis=0, tiled=True)]
    dot_general x6 -> x18, matrix products: 41.5 us -> 47.5 us  [the longest x4 10.2 us: expand(): jnp.einsum('pecd,edf->pecf', part, weight[:, cols], preferred_element_typ...]
    all_to_all x1 -> x2, waiting for transfers between devices: 112 us -> 107 us  [shards(): lax.all_to_all(outputs, 'ep', split_axis=0, concat_axis=0, tiled=True)]
  transfers between devices with their start and end apart: 4 -> 8, of which waited for: 4 -> 7; matrix products, arithmetic and copies ran while one was open for 5% -> 9% of each run, Pallas kernels for 0% -> 0%
where the time goes in v2:
time: 494 us; the launch traced here: 493 us
  waiting for transfers between devices  385 us (78%)
  matrix products  55 us (11%)
  starting transfers between devices  24.2 us (5%)
  between operations  13.5 us (3%)
  other arithmetic  8.72 us (2%)
  local copies, waits for them, and re-layouts  6.9 us (1%)
    all_gather x2, waiting for transfers between devices, gather_rows(): return lax.all_gather(part, ('ep', 'grp'), axis=0, tiled=True)  154 us
    all_to_all x2, waiting for transfers between devices, shards(): lax.all_to_all(outputs, 'ep', split_axis=0, concat_axis=0, tiled=True)  107 us
    all_to_all x2, waiting for transfers between devices, shards(): lax.all_to_all(blocks, 'ep', split_axis=0, concat_axis=0, tiled=True)  59.6 us
    all_gather x1, waiting for transfers between devices, gather_columns(): full = lax.all_gather(part, ('grp', 'ep'), axis=0, tiled=True)  42.8 us
    all_to_all x1, waiting for transfers between devices, shards(): lax.all_to_all(sent, 'ep', split_axis=0, concat_axis=0, tiled=True)  20.6 us
    dot_general x4, matrix products, expand(): jnp.einsum('pecd,edf->pecf', part, weight[:, cols], preferred_element_typ...  10.2 us
    dot_general x2, matrix products, shards(): result = jnp.dot(hidden, second_full[c], preferred_element_type=F32)  10.1 us
  transfers between devices with their start and end apart: 8, of which 7 were waited for; matrix products, arithmetic and copies ran while one was open for 9% of the time, Pallas kernels for 0%

profile of v2, /device:TPU:0, one launch (start us, length us, event | category | flops | bytes accessed | tf_op | source)
XLA Modules:
  0.0 493.1 jit_solution(17813380468563552824)
XLA Ops:
  15.1 7.3 %all-to-all-start = ((bf16[8,32,1280]{2,1,0:T(8,128)(2,1)}), bf16[8,32,1280]{2,1,0:T(8,128)(2,1)S(1)}, u32[]{:S(2)}, u32[]{:S(2)}) async-start(bf16[8,32,1280]{2,1,0:T(8,128)(2,1)} %bitcast), calls=%async_computation | async-start | bytes 1310720 | tf_op jit(solution)/shard_map/all_to_all | solution.py:61
  22.9 20.6 %all-to-all-done = bf16[8,32,1280]{2,1,0:T(8,128)(2,1)S(1)} async-done(((bf16[8,32,1280]{2,1,0:T(8,128)(2,1)}), bf16[8,32,1280]{2,1,0:T(8,128)(2,1)S(1)}, u32[]{:S(2)}, u32[]{:S(2)}) %all-to-all-start) | async-done | bytes 655392 | tf_op jit(solution)/shard_map/all_to_all | solution.py:61
  44.2 42.8 %all-gather.4.cloned.1.call-done = bf16[4608,640]{1,0:T(8,128)(2,1)} async-done(((bf16[144,640]{1,0:T(8,128)(2,1)}), bf16[4608,640]{1,0:T(8,128)(2,1)}) %all-gather.4.cloned.1.call-update) | async-done | bytes 5898256 | tf_op jit(solution)/shard_map/all_gather | solution.py:20
  87.0 3.4 fusion.84
  96.3 62.4 %all-gather.8.cloned.1.call-done = bf16[2560,1280]{1,0:T(8,128)(2,1)} async-done(((bf16[80,1280]{1,0:T(8,128)(2,1)}), bf16[2560,1280]{1,0:T(8,128)(2,1)}) %all-gather.8.cloned.1.call-update) | async-done | bytes 6553616 | tf_op jit(solution)/shard_map/all_gather | solution.py:28
  158.7 4.9 fusion.41
  163.7 2.4 convolution_convert_fusion.2
  166.1 4.0 all-to-all-start.2
  170.1 92.1 %all-gather.6.cloned.1.call-done = bf16[2560,1280]{1,0:T(8,128)(2,1)} async-done(((bf16[80,1280]{1,0:T(8,128)(2,1)}), bf16[2560,1280]{1,0:T(8,128)(2,1)}) %all-gather.6.cloned.1.call-update) | async-done | bytes 6553616 | tf_op jit(solution)/shard_map/all_gather | solution.py:28
  262.1 5.3 %fusion.38 = (f32[256]{0:T(256)S(1)}, bf16[256,1280]{1,0:T(8,128)(2,1)S(1)}) fusion(f32[1280]{0:T(1024)S(1)} %get-tuple-element.18, bf16[2560,1280]{1,0:T(8,128)(2,1)} %all-gather.6.cloned.1.call-done, bf16[256,640]{1,0:T(8,128)(2,1)} %copy-done.25, bf16[256,640]{1,0:T(8,128)(2,1)} %copy-done.24, bf16[256,640]{1,0:T(8,128)(2,1)} %copy-done.23, ...), kind=kOutput, calls=%fused_computation.57 | convolution fusion | flops 1684602624 | bytes 8525824 | tf_op jit(solution)/shard_map/dot_general | solution.py:88
  268.2 2.3 convolution_convert_fusion.3
  270.6 4.5 all-to-all-start.1
  275.7 59.6 %all-to-all-done.1 = bf16[8,1,128,1280]{3,2,1,0:T(8,128)(2,1)} async-done(((bf16[8,1,128,1280]{3,2,1,0:T(8,128)(2,1)}), bf16[8,1,128,1280]{3,2,1,0:T(8,128)(2,1)}, u32[]{:S(2)}, u32[]{:S(2)}) %all-to-all-start.1) | async-done | bytes 2621472 | tf_op jit(solution)/shard_map/all_to_all | solution.py:92
  335.3 2.5 fusion
  337.8 3.5 fusion.24
  341.3 3.3 fusion.22
  349.1 3.0 fusion.6
  352.1 3.6 all-to-all-start.3
  355.7 4.7 fusion.7
  360.4 54.9 %all-to-all-done.3 = bf16[8,1,128,1280]{3,2,1,0:T(8,128)(2,1)S(1)} async-done(((bf16[8,1,128,1280]{3,2,1,0:T(8,128)(2,1)}), bf16[8,1,128,1280]{3,2,1,0:T(8,128)(2,1)S(1)}, u32[]{:S(2)}, u32[]{:S(2)}) %all-to-all-start.3) | async-done | bytes 2621472 | tf_op jit(solution)/shard_map/all_to_all | solution.py:126
  415.4 4.6 all-to-all-start.4
  427.2 51.6 %all-to-all-done.4 = bf16[8,1,128,1280]{3,2,1,0:T(8,128)(2,1)} async-done(((bf16[8,1,128,1280]{3,2,1,0:T(8,128)(2,1)}), bf16[8,1,128,1280]{3,2,1,0:T(8,128)(2,1)}, u32[]{:S(2)}, u32[]{:S(2)}) %all-to-all-start.4) | async-done | bytes 2621472 | tf_op jit(solution)/shard_map/all_to_all | solution.py:126
  478.8 2.8 convolution_multiply_fusion.1
  482.7 2.7 fusion.14
  (98 shorter events, 30.6 us)
Async XLA Ops:
  6.5 15.9 %copy-start.14 = (s32[256,2]{0,1:T(2,128)S(1)}, s32[256,2]{0,1:T(2,128)}, u32[]{:S(2)}) copy-start(s32[256,2]{0,1:T(2,128)} %param.14) | copy-start | bytes 6148
  6.5 16.3 %copy-start.11 = (f32[2560]{0:T(1024)S(1)}, f32[2560]{0:T(1024)}, u32[]{:S(2)}) copy-start(f32[2560]{0:T(1024)} %param.16) | copy-start | bytes 30724
  6.5 16.3 %copy-start.12 = (f32[2560]{0:T(1024)S(1)}, f32[2560]{0:T(1024)}, u32[]{:S(2)}) copy-start(f32[2560]{0:T(1024)} %param.18) | copy-start | bytes 30724
  6.5 80.5 %all-gather.4.cloned.1.call-start = ((), (), s32[]{:S(2)}) async-start(), calls=%async_computation.5 | async-start | bytes 6082560 | tf_op jit(solution)/shard_map/all_gather | solution.py:20
  8.4 150.4 %all-gather.8.cloned.1.call-start = ((), (), s32[]{:S(2)}) async-start(), calls=%async_computation.7 | async-start | bytes 6758400 | tf_op jit(solution)/shard_map/all_gather | solution.py:28
  10.3 251.8 %all-gather.6.cloned.1.call-start = ((), (), s32[]{:S(2)}) async-start(), calls=%async_computation.6 | async-start | bytes 6758400 | tf_op jit(solution)/shard_map/all_gather | solution.py:28
  15.1 28.4 %all-to-all-start = ((bf16[8,32,1280]{2,1,0:T(8,128)(2,1)}), bf16[8,32,1280]{2,1,0:T(8,128)(2,1)S(1)}, u32[]{:S(2)}, u32[]{:S(2)}) async-start(bf16[8,32,1280]{2,1,0:T(8,128)(2,1)} %bitcast), calls=%async_computation | async-start | bytes 1310720 | tf_op jit(solution)/shard_map/all_to_all | solution.py:61
  22.8 140.8 %copy-start.2 = (pred[1024,256]{1,0:T(32,128)(4,1)}, pred[1024,256]{1,0:T(32,128)(4,1)S(1)}, u32[]{:S(2)}) copy-start(pred[1024,256]{1,0:T(32,128)(4,1)S(1)} %bitcast_compare_fusion) | copy-start | bytes 786436
  87.0 3.5 copy-start.15
  90.5 68.3 %copy-start.22 = (bf16[256,640]{1,0:T(8,128)(2,1)}, bf16[256,640]{1,0:T(8,128)(2,1)S(1)}, u32[]{:S(2)}) copy-start(bf16[256,640]{1,0:T(8,128)(2,1)S(1)} %fusion.84) | copy-start | bytes 983044
  92.4 66.3 %copy-start.23 = (bf16[256,640]{1,0:T(8,128)(2,1)}, bf16[256,640]{1,0:T(8,128)(2,1)S(1)}, u32[]{:S(2)}) copy-start(bf16[256,640]{1,0:T(8,128)(2,1)S(1)} %fusion.87) | copy-start | bytes 983044
  94.4 64.4 %copy-start.24 = (bf16[256,640]{1,0:T(8,128)(2,1)}, bf16[256,640]{1,0:T(8,128)(2,1)S(1)}, u32[]{:S(2)}) copy-start(bf16[256,640]{1,0:T(8,128)(2,1)S(1)} %fusion.90) | copy-start | bytes 983044
  96.3 67.3 %copy-start.25 = (bf16[256,640]{1,0:T(8,128)(2,1)}, bf16[256,640]{1,0:T(8,128)(2,1)S(1)}, u32[]{:S(2)}) copy-start(bf16[256,640]{1,0:T(8,128)(2,1)S(1)} %fusion.93) | copy-start | bytes 983044
  166.1 104.5 %all-to-all-start.2 = ((bf16[8,1,128,1280]{3,2,1,0:T(8,128)(2,1)}), bf16[8,1,128,1280]{3,2,1,0:T(8,128)(2,1)S(1)}, u32[]{:S(2)}, u32[]{:S(2)}) async-start(bf16[8,1,128,1280]{3,2,1,0:T(8,128)(2,1)} %bitcast.136), calls=%async_computation.2 | async-start | bytes 5242880 | tf_op jit(solution)/shard_map/all_to_all | solution.py:92
  262.1 6.1 %copy-start.3 = (pred[1024,256]{1,0:T(32,128)(4,1)S(1)}, pred[1024,256]{1,0:T(32,128)(4,1)}, u32[]{:S(2)}) copy-start(pred[1024,256]{1,0:T(32,128)(4,1)} %copy-done.2) | copy-start | bytes 786436
  270.6 4.5 copy-start.13
  270.6 64.7 %all-to-all-start.1 = ((bf16[8,1,128,1280]{3,2,1,0:T(8,128)(2,1)}), bf16[8,1,128,1280]{3,2,1,0:T(8,128)(2,1)}, u32[]{:S(2)}, u32[]{:S(2)}) async-start(bf16[8,1,128,1280]{3,2,1,0:T(8,128)(2,1)} %bitcast.137), calls=%async_computation.1 | async-start | bytes 5242880 | tf_op jit(solution)/shard_map/all_to_all | solution.py:92
  352.1 63.3 %all-to-all-start.3 = ((bf16[8,1,128,1280]{3,2,1,0:T(8,128)(2,1)}), bf16[8,1,128,1280]{3,2,1,0:T(8,128)(2,1)S(1)}, u32[]{:S(2)}, u32[]{:S(2)}) async-start(bf16[8,1,128,1280]{3,2,1,0:T(8,128)(2,1)} %fusion.6), calls=%async_computation.3 | async-start | bytes 5242880 | tf_op jit(solution)/shard_map/all_to_all | solution.py:126
  360.4 62.9 %copy-start.19 = (bf16[2560,8]{0,1:T(8,128)(2,1)S(1)}, bf16[2560,8]{0,1:T(8,128)(2,1)}, u32[]{:S(2)}) copy-start(bf16[2560,8]{0,1:T(8,128)(2,1)} %param.20) | copy-start | bytes 122884
  360.4 64.3 %copy-start.5 = (bf16[256,1280]{1,0:T(8,128)(2,1)S(1)}, bf16[256,1280]{1,0:T(8,128)(2,1)}, u32[]{:S(2)}) copy-start(bf16[256,1280]{1,0:T(8,128)(2,1)} %copy-done.4) | copy-start | bytes 1966084
  415.4 63.4 %all-to-all-start.4 = ((bf16[8,1,128,1280]{3,2,1,0:T(8,128)(2,1)}), bf16[8,1,128,1280]{3,2,1,0:T(8,128)(2,1)}, u32[]{:S(2)}, u32[]{:S(2)}) async-start(bf16[8,1,128,1280]{3,2,1,0:T(8,128)(2,1)} %fusion.7), calls=%async_computation.4 | async-start | bytes 5242880 | tf_op jit(solution)/shard_map/all_to_all | solution.py:126
  421.3 4.0 copy-start.10
  427.2 54.4 %copy-start.8 = (bf16[256,1280]{1,0:T(8,128)(2,1)S(1)}, bf16[256,1280]{1,0:T(8,128)(2,1)}, u32[]{:S(2)}) copy-start(bf16[256,1280]{1,0:T(8,128)(2,1)} %copy-done.7) | copy-start | bytes 1966084
  482.7 3.9 copy-start.1
  (10 other events, 21.0 us)
Sparse Core Ops, SparseCore 0:
  10.3 76.7 all-gather.3
  89.9 68.8 all-gather.7
  161.6 100.5 all-gather.5

commit v3 on v1

--- a/solution.py
+++ b/solution.py
@@ -1,6 +1,8 @@
 import jax
 import jax.numpy as jnp
 from jax import lax
+from jax.experimental import pallas as pl
+from jax.experimental.pallas import tpu as pltpu
 from jax.sharding import PartitionSpec as P
 
 EPSILON = 1e-06
@@ -12,12 +14,54 @@
     return jnp.dot(mask.astype(BF16), rows, preferred_element_type=F32).astype(BF16)
 
 
-def gather_columns(weight):
+def gather_columns(*weights):
     members = lax.axis_size("grp")
-    width = weight.shape[1] // members
-    part = lax.dynamic_slice_in_dim(weight, lax.axis_index("grp") * width, width, 1)
-    full = lax.all_gather(part, ("grp", "ep"), axis=0, tiled=True)
-    return full.reshape(members, -1, width)
+    width = weights[0].shape[1] // members
+    start = lax.axis_index("grp") * width
+    parts = [lax.dynamic_slice_in_dim(weight, start, width, 1) for weight in weights]
+    return lax.all_gather(jnp.concatenate(parts, axis=0), ("grp", "ep"), axis=0)
+
+
+def weight_kernel(start, rows_ref, weight_ref, out_ref):
+    blocks, _, depth = rows_ref.shape
+    span = pl.ds(start, depth)
+
+    def one(e):
+        return jnp.dot(rows_ref[e], weight_ref[e, span, :], preferred_element_type=F32)
+
+    if blocks <= 8:
+        out_ref[...] = sum(one(e) for e in range(blocks))
+    else:
+        out_ref[...] = jnp.zeros_like(out_ref)
+
+        @pl.loop(0, blocks)
+        def _(e):
+            out_ref[...] += one(e)
+
+
+def weight_dot(rows, gathered, start, depth):
+    blocks = lax.axis_size("ep")
+    total, height, width = gathered.shape
+    count = rows.shape[0]
+    rows = rows.reshape(count, blocks, depth).swapaxes(0, 1)
+    read = depth if start == 0 and depth % 16 == 0 else height
+    parts = total // blocks
+    return pl.pallas_call(
+        lambda *refs: weight_kernel(start, *refs),
+        grid=(parts,),
+        in_specs=[
+            pl.BlockSpec((blocks, count, depth), lambda g: (0, 0, 0)),
+            pl.BlockSpec((blocks, read, width), lambda g: (g, 0, 0)),
+        ],
+        out_specs=pl.BlockSpec((count, width), lambda g: (0, g)),
+        out_shape=jax.ShapeDtypeStruct((count, parts * width), F32),
+        compiler_params=pltpu.CompilerParams(vmem_limit_bytes=40 << 20),
+        cost_estimate=pl.CostEstimate(
+            flops=2 * count * parts * blocks * depth * width,
+            bytes_accessed=2 * parts * blocks * read * width,
+            transcendentals=0,
+        ),
+    )(rows, gathered)
 
 
 def shards(
@@ -37,8 +81,8 @@
     members = lax.axis_size("ep")
     row_count, vis = features.shape
     width = proj_in.shape[1]
-    first_full = gather_columns(proj_in)
-    second_full = gather_columns(proj_out)
+    gathered = gather_columns(proj_in, proj_out)
+    depth = proj_in.shape[0]
 
     index = jnp.arange(row_count, dtype=jnp.int32)
     rank = jnp.sum((token_position[None, :] < token_position[:, None]).astype(jnp.int32), axis=1)
@@ -52,11 +96,10 @@
     landing = (arrived[:, vis].astype(F32) * 16 + arrived[:, vis + 1].astype(F32)).astype(jnp.int32)
     patches = select_rows(landing[None, :] == index[:, None], arrived[:, :vis])
 
-    pre_act = jnp.einsum("rk,gkn->rgn", patches, first_full, preferred_element_type=F32)
-    pre_act = pre_act.reshape(row_count, width)
+    pre_act = weight_dot(patches, gathered, 0, depth)
     hidden = jax.nn.gelu(pre_act + bias_in, approximate=False).astype(BF16)
-    result = jnp.einsum("rk,gkn->rgn", hidden, second_full, preferred_element_type=F32)
-    tokens = (result.reshape(row_count, width) + bias_out).astype(BF16)
+    result = weight_dot(hidden, gathered, depth, proj_out.shape[0])
+    tokens = (result + bias_out).astype(BF16)
 
     wide = tokens.astype(F32)
     scale = lax.rsqrt(jnp.mean(wide * wide, axis=-1, keepdims=True) + EPSILON)

time: 496 us -> 454 us (0.915)
  waiting for transfers between devices: 261 us -> 233 us
  matrix products: 48.7 us -> 28.7 us
  local copies, waits for them, and re-layouts: 35.4 us -> 19.2 us
  Pallas kernels: 0 us -> 15.8 us
  other arithmetic: 2.74 us -> 9.87 us
    all_gather x2 -> x1, waiting for transfers between devices: 129 us -> 91.7 us  [gather_columns(): return lax.all_gather(jnp.concatenate(parts, axis=0), ('grp', 'ep'), axis=0)]
    dot_general x2 -> x0, local copies, waits for them, and re-layouts: 26.6 us -> none  [the longest x1 17.7 us: shards(): jnp.einsum('rk,gkn->rgn', hidden, second_full, preferred_element_type=F32)]
    dot_general x1 -> x0, matrix products: 15.8 us -> none  [shards(): jnp.einsum('rk,gkn->rgn', hidden, second_full, preferred_element_type=F32)]
    pallas_call x0 -> x2, Pallas kernels: none -> 15.8 us  [weight_dot(): pl.pallas_call(lambda *refs: weight_kernel(start, *refs), grid=(parts,),...]
    all_to_all x1, waiting for transfers between devices: 20.2 us -> 28.6 us  [shards(): lax.all_to_all(sent, 'ep', split_axis=0, concat_axis=0, tiled=True)]
    convert_element_type x0 -> x1, other arithmetic: none -> 6.56 us  [shards(): hidden = jax.nn.gelu(pre_act + bias_in, approximate=False).astype(BF16)]
  transfers between devices with their start and end apart: 4 -> 3, of which waited for: 4 -> 3; matrix products, arithmetic and copies ran while one was open for 5% -> 3% of each run, Pallas kernels for 0% -> 0%
where the time goes in v3:
time: 454 us; the launch traced here: 453 us
  waiting for transfers between devices  233 us (51%)
  blocking collectives  120 us (26%)
  matrix products  28.7 us (6%)
  local copies, waits for them, and re-layouts  19.2 us (4%)
  Pallas kernels  15.8 us (3%)
  between operations  13.7 us (3%)
  starting transfers between devices  12.3 us (3%)
  other arithmetic  9.87 us (2%)
    all_to_all x1, blocking collectives, shards(): lax.all_to_all(blocks, 'ep', split_axis=0, concat_axis=0, tiled=True)  120 us
    all_to_all x1, waiting for transfers between devices, shards(): lax.all_to_all(outputs, 'ep', split_axis=0, concat_axis=0, tiled=True)  113 us
    all_gather x1, waiting for transfers between devices, gather_columns(): return lax.all_gather(jnp.concatenate(parts, axis=0), ('grp', 'ep'), axis=0)  91.7 us
    all_to_all x1, waiting for transfers between devices, shards(): lax.all_to_all(sent, 'ep', split_axis=0, concat_axis=0, tiled=True)  28.6 us
    pallas_call x2, Pallas kernels, weight_dot(): pl.pallas_call(lambda *refs: weight_kernel(start, *refs), grid=(parts,),...  15.8 us
    dot_general x1, matrix products, shards(): jnp.einsum('pecf,efd->pecd', activated, w_down, preferred_element_type=F32)  10.3 us
    dot_general x2, matrix products, shards(): row = jnp.dot(picked.astype(BF16), returned, preferred_element_type=F32)  9.49 us
  transfers between devices with their start and end apart: 3, of which 3 were waited for; matrix products, arithmetic and copies ran while one was open for 3% of the time, Pallas kernels for 0%

profile of v3, /device:TPU:0, one launch (start us, length us, event | category | flops | bytes accessed | tf_op | source)
XLA Modules:
  0.0 452.8 jit_solution(10450075386748933974)
XLA Ops:
  6.6 1.2 constant_dynamic-slice_fusion
  11.2 7.3 %all-to-all-start = ((bf16[8,32,1280]{2,1,0:T(8,128)(2,1)}), bf16[8,32,1280]{2,1,0:T(8,128)(2,1)S(1)}, u32[]{:S(2)}, u32[]{:S(2)}) async-start(bf16[8,32,1280]{2,1,0:T(8,128)(2,1)} %bitcast.124), calls=%async_computation | async-start | bytes 1310720 | tf_op jit(solution)/shard_map/all_to_all | solution.py:95
  19.0 28.6 %all-to-all-done = bf16[8,32,1280]{2,1,0:T(8,128)(2,1)S(1)} async-done(((bf16[8,32,1280]{2,1,0:T(8,128)(2,1)}), bf16[8,32,1280]{2,1,0:T(8,128)(2,1)S(1)}, u32[]{:S(2)}, u32[]{:S(2)}) %all-to-all-start) | async-done | bytes 655392 | tf_op jit(solution)/shard_map/all_to_all | solution.py:95
  48.2 1.5 copy.54
  49.8 1.5 copy.55
  53.1 1.4 copy.46
  54.6 1.3 copy.47
  55.8 91.7 %all-gather.3.cloned.1.call-done = bf16[14848,640]{1,0:T(8,128)(2,1)} async-done(((bf16[464,640]{1,0:T(8,128)(2,1)}), bf16[14848,640]{1,0:T(8,128)(2,1)}) %all-gather.3.cloned.1.call-update) | async-done | bytes 19005456 | tf_op jit(solution)/shard_map/all_gather | solution.py:22
  147.5 1.2 copy-done.3
  148.8 5.9 %shard_map.118 = f32[256,2560]{1,0:T(8,128)S(1)} custom-call(bf16[8,256,144]{2,1,0:T(8,128)(2,1)S(1)} %bitcast.116, bf16[32,464,640]{2,1,0:T(8,128)(2,1)} %bitcast.117), custom_call_target="tpu_custom_call" | custom-call | flops 1509949440 | bytes 5898240 | tf_op jit(solution)/shard_map/pallas_call | solution.py:49
  154.6 6.6 %fusion.10 = bf16[256,2560]{1,0:T(8,128)(2,1)} fusion(f32[256,2560]{1,0:T(8,128)S(1)} %shard_map.118, f32[2560]{0:T(1024)S(1)} %copy-done.8), kind=kLoop, calls=%fused_computation.17 | loop fusion | flops 43253760 | bytes 3942400 | tf_op jit(solution)/shard_map/convert_element_type | solution.py:100
  161.2 2.4 copy.48
  163.6 2.5 copy.49
  166.2 1.4 copy-done.2
  167.6 10.0 %shard_map.119 = f32[256,2560]{1,0:T(8,128)S(1)} custom-call(bf16[8,256,320]{2,1,0:T(8,128)(2,1)S(1)} %bitcast.115, bf16[32,464,640]{2,1,0:T(8,128)(2,1)} %bitcast.118), custom_call_target="tpu_custom_call" | custom-call | flops 3355443200 | bytes 19005440 | tf_op jit(solution)/shard_map/pallas_call | solution.py:49
  178.3 1.7 convolution_convert_fusion
  180.0 119.8 %all_to_all.22 = bf16[8,1,128,2560]{3,2,1,0:T(8,128)(2,1)S(1)} all-to-all(bf16[8,1,128,2560]{3,2,1,0:T(8,128)(2,1)S(1)} %bitcast.119), channel_id=1, replica_groups=mesh['grp'=4,'ep'=8] {'ep'}, dimensions={0} | all-to-all | bytes 10485760 | tf_op jit(solution)/shard_map/all_to_all | solution.py:126
  299.8 2.4 copy-done.4
  302.2 4.2 fusion.2
  306.4 10.3 %fusion.4 = bf16[8,1,128,2560]{3,2,1,0:T(8,128)(2,1)} fusion(bf16[1,512,2560]{2,1,0:T(8,128)(2,1)S(1)} %copy-done, bf16[1,2560,512]{2,1,0:T(8,128)(2,1)} %param.22, bf16[8,1,128,2560]{3,2,1,0:T(8,128)(2,1)} %copy-done.4, f32[8,128,512]{2,1,0:T(8,128)} %fusion.2), kind=kOutput, calls=%fused_computation.6 | convolution fusion | flops 5374476288 | bytes 17825792 | tf_op jit(solution)/shard_map/pecf,efd->pecd/dot_general | solution.py:130
  316.7 5.0 %all-to-all-start.2 = ((bf16[8,1,128,2560]{3,2,1,0:T(8,128)(2,1)}), bf16[8,1,128,2560]{3,2,1,0:T(8,128)(2,1)}, u32[]{:S(2)}, u32[]{:S(2)}) async-start(bf16[8,1,128,2560]{3,2,1,0:T(8,128)(2,1)} %fusion.4), calls=%async_computation.2 | async-start | bytes 10485760 | tf_op jit(solution)/shard_map/all_to_all | solution.py:131
  323.3 113.2 %all-to-all-done.2 = bf16[8,1,128,2560]{3,2,1,0:T(8,128)(2,1)} async-done(((bf16[8,1,128,2560]{3,2,1,0:T(8,128)(2,1)}), bf16[8,1,128,2560]{3,2,1,0:T(8,128)(2,1)}, u32[]{:S(2)}, u32[]{:S(2)}) %all-to-all-start.2) | async-done | bytes 5242912 | tf_op jit(solution)/shard_map/all_to_all | solution.py:131
  436.5 4.1 convolution_multiply_fusion
  440.6 5.4 %fusion.7 = bf16[256,2560]{1,0:T(8,128)(2,1)} fusion(f32[256,2560]{1,0:T(8,128)S(1)} %convolution_multiply_fusion, bf16[1024,2560]{1,0:T(8,128)(2,1)} %bitcast.35, bf16[256,2560]{1,0:T(8,128)(2,1)S(1)} %copy-done.7, f32[256]{0:T(256)S(1)} %bitcast.128, pred[32,8,8,128]{3,2,1,0:T(8,128)(4,1)S(1)} %bitcast.125), kind=kOutput, calls=%fused_computation.14 | convolution fusion | flops 1345454080 | bytes 10748928 | tf_op jit(solution)/shard_map/dot_general | solution.py:137
  (57 shorter events, 8.6 us)
Async XLA Ops:
  6.5 299.9 %copy-start = (bf16[1,512,2560]{2,1,0:T(8,128)(2,1)S(1)}, bf16[1,512,2560]{2,1,0:T(8,128)(2,1)}, u32[]{:S(2)}) copy-start(bf16[1,512,2560]{2,1,0:T(8,128)(2,1)} %param.23) | copy-start | bytes 7864324
  6.5 3.1 copy-start.11
  6.5 3.5 copy-start.15
  6.5 141.0 %all-gather.3.cloned.1.call-start = ((), (), s32[]{:S(2)}) async-start(), calls=%async_computation.3 | async-start | bytes 19599360 | tf_op jit(solution)/shard_map/all_gather | solution.py:22
  7.7 10.8 %copy-start.12 = (s32[256,2]{0,1:T(2,128)S(1)}, s32[256,2]{0,1:T(2,128)}, u32[]{:S(2)}) copy-start(s32[256,2]{0,1:T(2,128)} %param.14) | copy-start | bytes 6148
  11.2 36.3 %all-to-all-start = ((bf16[8,32,1280]{2,1,0:T(8,128)(2,1)}), bf16[8,32,1280]{2,1,0:T(8,128)(2,1)S(1)}, u32[]{:S(2)}, u32[]{:S(2)}) async-start(bf16[8,32,1280]{2,1,0:T(8,128)(2,1)} %bitcast.124), calls=%async_computation | async-start | bytes 1310720 | tf_op jit(solution)/shard_map/all_to_all | solution.py:95
  147.5 1.2 copy-start.3
  148.8 5.9 %copy-start.8 = (f32[2560]{0:T(1024)S(1)}, f32[2560]{0:T(1024)}, u32[]{:S(2)}) copy-start(f32[2560]{0:T(1024)} %param.16) | copy-start | bytes 30724
  166.2 1.4 copy-start.2
  167.6 10.0 %copy-start.9 = (f32[2560]{0:T(1024)S(1)}, f32[2560]{0:T(1024)}, u32[]{:S(2)}) copy-start(f32[2560]{0:T(1024)} %param.18) | copy-start | bytes 30724
  177.6 0.7 copy-start.10
  178.0 2.0 copy-start.5
  180.0 122.2 %copy-start.14 = (bf16[1,2560,512]{2,1,0:T(8,128)(2,1)S(1)}, bf16[1,2560,512]{2,1,0:T(8,128)(2,1)}, u32[]{:S(2)}) copy-start(bf16[1,2560,512]{2,1,0:T(8,128)(2,1)} %param.21) | copy-start | bytes 7864324
  299.8 2.4 copy-start.4
  316.7 6.0 %copy-start.6 = (bf16[256,2560]{1,0:T(8,128)(2,1)S(1)}, bf16[256,2560]{1,0:T(8,128)(2,1)}, u32[]{:S(2)}) copy-start(bf16[256,2560]{1,0:T(8,128)(2,1)} %copy-done.5) | copy-start | bytes 3932164
  316.7 6.0 %copy-start.16 = (bf16[2560,8]{0,1:T(8,128)(2,1)S(1)}, bf16[2560,8]{0,1:T(8,128)(2,1)}, u32[]{:S(2)}) copy-start(bf16[2560,8]{0,1:T(8,128)(2,1)} %param.20) | copy-start | bytes 122884
  316.7 119.7 %all-to-all-start.2 = ((bf16[8,1,128,2560]{3,2,1,0:T(8,128)(2,1)}), bf16[8,1,128,2560]{3,2,1,0:T(8,128)(2,1)}, u32[]{:S(2)}, u32[]{:S(2)}) async-start(bf16[8,1,128,2560]{3,2,1,0:T(8,128)(2,1)} %fusion.4), calls=%async_computation.2 | async-start | bytes 10485760 | tf_op jit(solution)/shard_map/all_to_all | solution.py:131
  321.7 1.5 copy-start.13
  436.5 4.1 copy-start.7
  440.6 5.4 %copy-start.1 = (bf16[1,512,2560]{2,1,0:T(8,128)(2,1)S(1)}, bf16[1,512,2560]{2,1,0:T(8,128)(2,1)}, u32[]{:S(2)}) copy-start(bf16[1,512,2560]{2,1,0:T(8,128)(2,1)} %param.23) | copy-start | bytes 7864324
Sparse Core Ops, SparseCore 0:
  10.2 137.2 all-gather.2

commit v4 on v3

--- a/solution.py
+++ b/solution.py
@@ -84,6 +84,8 @@
     gathered = gather_columns(proj_in, proj_out)
     depth = proj_in.shape[0]
 
+    far = lax.axis_size("ep") // 2
+    far_ids = lax.ppermute(expert_ids, "ep", [(i, (i + far) % members) for i in range(members)])
     index = jnp.arange(row_count, dtype=jnp.int32)
     rank = jnp.sum((token_position[None, :] < token_position[:, None]).astype(jnp.int32), axis=1)
     local = token_position % row_count
@@ -104,39 +106,69 @@
     wide = tokens.astype(F32)
     scale = lax.rsqrt(jnp.mean(wide * wide, axis=-1, keepdims=True) + EPSILON)
     normed = (wide * scale * norm_gain).astype(BF16)
+    half = members // 2
+    swap = [(i, (i + half) % members) for i in range(members)]
+    groups = [list(range(half)), list(range(half, members))]
     experts = router.shape[1]
+    near = experts // 2
+    first_near = lax.axis_index("ep") // half * near
     top_count = expert_ids.shape[1]
     capacity = 2 * row_count * top_count // experts
     local_experts = w_gate.shape[0]
-    logits = jnp.dot(normed, router, preferred_element_type=F32)
     numbers = jnp.arange(experts, dtype=jnp.int32)
-    chosen_mask = expert_ids[:, :, None] == numbers[None, None, :]
-    chosen = jnp.sum(jnp.where(chosen_mask, logits[:, None, :], 0.0), axis=2)
-    first_gate = jax.nn.sigmoid(chosen[:, 0] - chosen[:, 1])
-    gates = (first_gate, 1.0 - first_gate)
+    slots = jnp.arange(capacity, dtype=jnp.int32)
+    earlier = (index[None, :] < index[:, None]).astype(BF16)
 
-    named = jnp.any(chosen_mask, axis=1)
-    earlier = (index[None, :] < index[:, None]).astype(BF16)
-    before = jnp.dot(earlier, named.astype(BF16), preferred_element_type=F32).astype(jnp.int32)
-    place = jnp.where(named, before, -1)
-    slots = jnp.arange(capacity, dtype=jnp.int32)
-    filled = place.T[:, None, :] == slots[None, :, None]
-    blocks = select_rows(filled.reshape(experts * capacity, row_count), normed)
-    blocks = blocks.reshape(members, local_experts, capacity, width)
-    received = lax.all_to_all(blocks, "ep", split_axis=0, concat_axis=0, tiled=True)
-    gate_part = jnp.einsum("pecd,edf->pecf", received, w_gate, preferred_element_type=F32)
-    up_part = jnp.einsum("pecd,edf->pecf", received, w_up, preferred_element_type=F32)
-    activated = (jax.nn.silu(gate_part) * up_part).astype(BF16)
-    outputs = jnp.einsum("pecf,efd->pecd", activated, w_down, preferred_element_type=F32).astype(BF16)
-    returned = lax.all_to_all(outputs, "ep", split_axis=0, concat_axis=0, tiled=True)
-    returned = returned.reshape(experts * capacity, width)
-    total = 0.0
-    for choice in range(top_count):
-        slot = jnp.where(chosen_mask[:, choice], before, -1)
-        picked = (slot[:, :, None] == slots[None, None, :]).reshape(row_count, experts * capacity)
-        row = jnp.dot(picked.astype(BF16), returned, preferred_element_type=F32)
-        total = total + gates[choice][:, None] * row
-    return (wide + total).astype(BF16)
+    def exchange(blocks):
+        return lax.all_to_all(
+            blocks, "ep", split_axis=0, concat_axis=0, axis_index_groups=groups, tiled=True
+        )
+
+    def plan(ids):
+        chosen_mask = ids[:, :, None] == numbers[None, None, :]
+        named = jnp.any(chosen_mask, axis=1)
+        before = jnp.dot(earlier, named.astype(BF16), preferred_element_type=F32).astype(jnp.int32)
+        return chosen_mask, named, before
+
+    def dispatch(routes, rows):
+        _, named, before = routes
+        place = lax.dynamic_slice_in_dim(jnp.where(named, before, -1).T, first_near, near, 0)
+        filled = place[:, None, :] == slots[None, :, None]
+        blocks = select_rows(filled.reshape(near * capacity, row_count), rows)
+        return exchange(blocks.reshape(half, local_experts, capacity, width))
+
+    def run(received):
+        gate_part = jnp.einsum("pecd,edf->pecf", received, w_gate, preferred_element_type=F32)
+        up_part = jnp.einsum("pecd,edf->pecf", received, w_up, preferred_element_type=F32)
+        activated = (jax.nn.silu(gate_part) * up_part).astype(BF16)
+        outputs = jnp.einsum("pecf,efd->pecd", activated, w_down, preferred_element_type=F32)
+        return exchange(outputs.astype(BF16)).reshape(near * capacity, width)
+
+    def combine(routes, rows, returned):
+        chosen_mask, _, before = routes
+        logits = jnp.dot(rows, router, preferred_element_type=F32)
+        chosen = jnp.sum(jnp.where(chosen_mask, logits[:, None, :], 0.0), axis=2)
+        first_gate = jax.nn.sigmoid(chosen[:, 0] - chosen[:, 1])
+        gates = (first_gate, 1.0 - first_gate)
+        total = 0.0
+        for choice in range(top_count):
+            slot = jnp.where(chosen_mask[:, choice], before, -1)
+            slot = lax.dynamic_slice_in_dim(slot, first_near, near, 1)
+            picked = (slot[:, :, None] == slots[None, None, :]).reshape(row_count, near * capacity)
+            row = jnp.dot(picked.astype(BF16), returned, preferred_element_type=F32)
+            total = total + gates[choice][:, None] * row
+        return total
+
+    own_plan = plan(expert_ids)
+    far_plan = plan(far_ids)
+    far_rows = lax.ppermute(normed, "ep", swap)
+    own_received = dispatch(own_plan, normed)
+    far_rows, own_received = lax.optimization_barrier((far_rows, own_received))
+    far_received = dispatch(far_plan, far_rows)
+    far_total = combine(far_plan, far_rows, run(far_received)).astype(BF16)
+    far_back = lax.ppermute(far_total, "ep", swap)
+    total = combine(own_plan, normed, run(own_received))
+    return (wide + total + far_back.astype(F32)).astype(BF16)
 
 
 def solution(mesh):

time: 454 us -> 412 us (0.907)
  blocking collectives: 120 us -> 34.3 us
  matrix products: 28.7 us -> 45 us
  starting transfers between devices: 12.3 us -> 25.8 us
  waiting for transfers between devices: 233 us -> 245 us
    all_to_all x1, blocking collectives: 120 us -> 34.3 us  [exchange(): lax.all_to_all(blocks, 'ep', split_axis=0, concat_axis=0, axis_index_grou...]
    ppermute x0 -> x3, waiting for transfers between devices: none -> 70.8 us  [the longest x1 55.6 us: shards(): far_rows = lax.ppermute(normed, 'ep', swap)]
    all_to_all x1 -> x3, waiting for transfers between devices: 113 us -> 55.9 us  [exchange(): lax.all_to_all(blocks, 'ep', split_axis=0, concat_axis=0, axis_index_grou...]
    dot_general x6 -> x12, matrix products: 24.7 us -> 38.1 us  [the longest x2 14.6 us: run(): jnp.einsum('pecf,efd->pecd', activated, w_down, preferred_element_type=F32)]
    all_to_all x1 -> x3, starting transfers between devices: 4.97 us -> 13.8 us  [exchange(): lax.all_to_all(blocks, 'ep', split_axis=0, concat_axis=0, axis_index_grou...]
    ppermute x0 -> x3, starting transfers between devices: none -> 8.11 us  [the longest x1 4.13 us: shards(): lax.ppermute(expert_ids, 'ep', [(i, (i + far) % members) for i in range(m...]
  transfers between devices with their start and end apart: 3 -> 8, of which waited for: 3 -> 7; matrix products, arithmetic and copies ran while one was open for 3% -> 9% of each run, Pallas kernels for 0% -> 0%
where the time goes in v4:
time: 412 us; the launch traced here: 411 us
  waiting for transfers between devices  245 us (59%)
  matrix products  45 us (11%)
  blocking collectives  34.3 us (8%)
  starting transfers between devices  25.8 us (6%)
  local copies, waits for them, and re-layouts  19.5 us (5%)
  Pallas kernels  15.8 us (4%)
  between operations  13.7 us (3%)
  other arithmetic  11.7 us (3%)
    all_gather x1, waiting for transfers between devices, gather_columns(): return lax.all_gather(jnp.concatenate(parts, axis=0), ('grp', 'ep'), axis=0)  91.2 us
    all_to_all x3, waiting for transfers between devices, exchange(): lax.all_to_all(blocks, 'ep', split_axis=0, concat_axis=0, axis_index_grou...  55.9 us
    ppermute x1, waiting for transfers between devices, shards(): far_rows = lax.ppermute(normed, 'ep', swap)  55.6 us
    all_to_all x1, blocking collectives, exchange(): lax.all_to_all(blocks, 'ep', split_axis=0, concat_axis=0, axis_index_grou...  34.3 us
    all_to_all x1, waiting for transfers between devices, shards(): lax.all_to_all(sent, 'ep', split_axis=0, concat_axis=0, tiled=True)  27 us
    pallas_call x2, Pallas kernels, weight_dot(): pl.pallas_call(lambda *refs: weight_kernel(start, *refs), grid=(parts,),...  15.8 us
    ppermute x1, waiting for transfers between devices, shards(): far_back = lax.ppermute(far_total, 'ep', swap)  15.2 us
    dot_general x2, matrix products, run(): jnp.einsum('pecf,efd->pecd', activated, w_down, preferred_element_type=F32)  14.6 us
  transfers between devices with their start and end apart: 8, of which 7 were waited for; matrix products, arithmetic and copies ran while one was open for 9% of the time, Pallas kernels for 0%

profile of v4, /device:TPU:0, one launch (start us, length us, event | category | flops | bytes accessed | tf_op | source)
XLA Modules:
  0.0 410.9 jit_solution(10006257209930647100)
XLA Ops:
  9.7 4.1 %collective-permute-start.1 = (s32[256,2]{0,1:T(2,128)S(1)}, s32[256,2]{0,1:T(2,128)S(1)}, u32[]{:S(2)}, u32[]{:S(2)}) collective-permute-start(s32[256,2]{0,1:T(2,128)S(1)} %copy-done.13), channel_id=1, source_target_pairs={{0,4},{1,5},{2,6},{3,7},{4,0},{5,1},{6,2},{7,3},{8,12},{9,13},{10,... | collective-permute-start | bytes 6152 | tf_op jit(solution)/shard_map/ppermute | solution.py:88
  15.3 3.8 all-to-all-start
  21.4 27.0 %all-to-all-done = bf16[8,32,1280]{2,1,0:T(8,128)(2,1)S(1)} async-done(((bf16[8,32,1280]{2,1,0:T(8,128)(2,1)}), bf16[8,32,1280]{2,1,0:T(8,128)(2,1)S(1)}, u32[]{:S(2)}, u32[]{:S(2)}) %all-to-all-start) | async-done | bytes 655392 | tf_op jit(solution)/shard_map/all_to_all | solution.py:97
  56.7 91.2 %all-gather.3.cloned.1.call-done = bf16[14848,640]{1,0:T(8,128)(2,1)} async-done(((bf16[464,640]{1,0:T(8,128)(2,1)}), bf16[14848,640]{1,0:T(8,128)(2,1)}) %all-gather.3.cloned.1.call-update) | async-done | bytes 19005456 | tf_op jit(solution)/shard_map/all_gather | solution.py:22
  149.1 5.9 %shard_map.118 = f32[256,2560]{1,0:T(8,128)S(1)} custom-call(bf16[8,256,144]{2,1,0:T(8,128)(2,1)S(1)} %bitcast.196, bf16[32,464,640]{2,1,0:T(8,128)(2,1)} %bitcast.197), custom_call_target="tpu_custom_call" | custom-call | flops 1509949440 | bytes 5898240 | tf_op jit(solution)/shard_map/pallas_call | solution.py:49
  155.0 6.6 %fusion.8 = bf16[256,2560]{1,0:T(8,128)(2,1)} fusion(f32[256,2560]{1,0:T(8,128)S(1)} %shard_map.118, f32[2560]{0:T(1024)S(1)} %copy-done.9), kind=kLoop, calls=%fused_computation.19 | loop fusion | flops 43253760 | bytes 3942400 | tf_op jit(solution)/shard_map/convert_element_type | solution.py:102
  164.0 2.6 copy.63
  168.0 10.0 %shard_map.119 = f32[256,2560]{1,0:T(8,128)S(1)} custom-call(bf16[8,256,320]{2,1,0:T(8,128)(2,1)S(1)} %bitcast.195, bf16[32,464,640]{2,1,0:T(8,128)(2,1)} %bitcast.198), custom_call_target="tpu_custom_call" | custom-call | flops 3355443200 | bytes 19005440 | tf_op jit(solution)/shard_map/pallas_call | solution.py:49
  181.4 4.6 %all-to-all-start.1 = ((bf16[4,1,128,2560]{3,2,1,0:T(8,128)(2,1)}), bf16[4,1,128,2560]{3,2,1,0:T(8,128)(2,1)}, u32[]{:S(2)}, u32[]{:S(2)}) async-start(bf16[4,1,128,2560]{3,2,1,0:T(8,128)(2,1)} %bitcast.199), calls=%async_computation.1 | async-start | bytes 5242880 | tf_op jit(solution)/shard_map/all_to_all | solution.py:123
  187.6 55.6 %collective-permute-done = bf16[256,2560]{1,0:T(8,128)(2,1)} collective-permute-done((bf16[256,2560]{1,0:T(8,128)(2,1)}, bf16[256,2560]{1,0:T(8,128)(2,1)}, u32[]{:S(2)}, u32[]{:S(2)}) %collective-permute-start) | collective-permute-done | bytes 1310752 | tf_op jit(solution)/shard_map/ppermute | solution.py:164
  247.5 34.3 %all_to_all.32 = bf16[4,1,128,2560]{3,2,1,0:T(8,128)(2,1)S(1)} all-to-all(bf16[4,1,128,2560]{3,2,1,0:T(8,128)(2,1)S(1)} %bitcast.200), channel_id=1, replica_groups={{0,1,2,3},{4,5,6,7},{8,9,10,11},{12,13,14,15},{16,17,18,19},{20,21,22,2..., dimensions={0} | all-to-all | bytes 5242880 | tf_op jit(solution)/shard_map/all_to_all | solution.py:123
  283.4 2.5 fusion.43
  285.9 7.3 %fusion.4 = bf16[4,1,128,2560]{3,2,1,0:T(8,128)(2,1)} fusion(bf16[1,512,2560]{2,1,0:T(8,128)(2,1)S(1)} %copy-done, bf16[1,2560,512]{2,1,0:T(8,128)(2,1)} %param.22, bf16[4,1,128,2560]{3,2,1,0:T(8,128)(2,1)} %copy-done.7, f32[4,1,128,512]{3,2,0,1:T(8,128)} %fusion.43), kind=kOutput, calls=%fused_computation.12 | convolution fusion | flops 2687238144 | bytes 11534336 | tf_op jit(solution)/shard_map/pecf,efd->pecd/dot_general | solution.py:144
  293.3 4.7 %all-to-all-start.4 = ((bf16[4,1,128,2560]{3,2,1,0:T(8,128)(2,1)}), bf16[4,1,128,2560]{3,2,1,0:T(8,128)(2,1)}, u32[]{:S(2)}, u32[]{:S(2)}) async-start(bf16[4,1,128,2560]{3,2,1,0:T(8,128)(2,1)} %fusion.4), calls=%async_computation.4 | async-start | bytes 5242880 | tf_op jit(solution)/shard_map/all_to_all | solution.py:123
  298.0 5.0 %fusion.33 = f32[4,1,128,512]{3,2,0,1:T(8,128)} fusion(bf16[1,2560,512]{2,1,0:T(8,128)(2,1)} %param.21, bf16[4,1,128,2560]{3,2,1,0:T(8,128)(2,1)} %all-to-all-done.1), kind=kOutput, calls=%fused_computation.56 | convolution fusion | flops 1342177280 | bytes 6291456 | tf_op jit(solution)/shard_map/pecd,edf->pecf/dot_general | solution.py:141
  303.0 7.2 %fusion.3 = bf16[4,1,128,2560]{3,2,1,0:T(8,128)(2,1)} fusion(bf16[1,512,2560]{2,1,0:T(8,128)(2,1)S(1)} %copy-done, f32[4,1,128,512]{3,2,0,1:T(8,128)} %fusion.33, bf16[1,2560,512]{2,1,0:T(8,128)(2,1)} %param.22, bf16[4,1,128,2560]{3,2,1,0:T(8,128)(2,1)} %all-to-all-done.1), kind=kOutput, calls=%fused_computation.11 | convolution fusion | flops 2687238144 | bytes 11534336 | tf_op jit(solution)/shard_map/pecf,efd->pecd/dot_general | solution.py:144
  310.3 16.1 %all-to-all-done.4 = bf16[4,1,128,2560]{3,2,1,0:T(8,128)(2,1)} async-done(((bf16[4,1,128,2560]{3,2,1,0:T(8,128)(2,1)}), bf16[4,1,128,2560]{3,2,1,0:T(8,128)(2,1)}, u32[]{:S(2)}, u32[]{:S(2)}) %all-to-all-start.4) | async-done | bytes 2621472 | tf_op jit(solution)/shard_map/all_to_all | solution.py:123
  326.4 4.6 %all-to-all-start.2 = ((bf16[4,1,128,2560]{3,2,1,0:T(8,128)(2,1)}), bf16[4,1,128,2560]{3,2,1,0:T(8,128)(2,1)}, u32[]{:S(2)}, u32[]{:S(2)}) async-start(bf16[4,1,128,2560]{3,2,1,0:T(8,128)(2,1)} %fusion.3), calls=%async_computation.2 | async-start | bytes 5242880 | tf_op jit(solution)/shard_map/all_to_all | solution.py:123
  334.1 2.6 convolution_multiply_fusion.1
  336.7 3.9 fusion.5
  344.2 37.6 %all-to-all-done.2 = bf16[4,1,128,2560]{3,2,1,0:T(8,128)(2,1)} async-done(((bf16[4,1,128,2560]{3,2,1,0:T(8,128)(2,1)}), bf16[4,1,128,2560]{3,2,1,0:T(8,128)(2,1)}, u32[]{:S(2)}, u32[]{:S(2)}) %all-to-all-start.2) | async-done | bytes 2621472 | tf_op jit(solution)/shard_map/all_to_all | solution.py:123
  381.8 2.7 convolution_multiply_fusion.3
  384.5 15.2 %collective-permute-done.2 = bf16[256,2560]{1,0:T(8,128)(2,1)} collective-permute-done((bf16[256,2560]{1,0:T(8,128)(2,1)}, bf16[256,2560]{1,0:T(8,128)(2,1)}, u32[]{:S(2)}, u32[]{:S(2)}) %collective-permute-start.2) | collective-permute-done | bytes 1310752 | tf_op jit(solution)/shard_map/ppermute | solution.py:169
  399.7 4.3 %add_convert_fusion = bf16[256,2560]{1,0:T(8,128)(2,1)} fusion(bf16[256,2560]{1,0:T(8,128)(2,1)} %collective-permute-done.2, f32[256,2560]{1,0:T(8,128)S(1)} %convolution_multiply_fusion.3, bf16[512,2560]{1,0:T(8,128)(2,1)} %bitcast.35, f32[256]{0:T(256)S(1)} %bitcast.213, bf16[256,2560]{1,0:T(8,128)(2,1)S(1)} %copy-done.4, ...), kind=kOutput, calls=%fused_computation.37 | convolution fusion | flops 675676160 | bytes 9307136 | tf_op jit(solution)/shard_map/dot_general | solution.py:158
  (89 shorter events, 37.6 us)
Async XLA Ops:
  6.5 279.4 %copy-start = (bf16[1,512,2560]{2,1,0:T(8,128)(2,1)S(1)}, bf16[1,512,2560]{2,1,0:T(8,128)(2,1)}, u32[]{:S(2)}) copy-start(bf16[1,512,2560]{2,1,0:T(8,128)(2,1)} %param.23) | copy-start | bytes 7864324
  6.5 3.1 copy-start.13
  6.5 7.3 %copy-start.12 = (s32[256]{0:T(256)S(1)}, s32[256]{0:T(256)}, u32[]{:S(2)}) copy-start(s32[256]{0:T(256)} %param.13) | copy-start | bytes 3076
  6.5 7.6 %copy-start.18 = (bf16[256,1152]{1,0:T(8,128)(2,1)S(1)}, bf16[256,1152]{1,0:T(8,128)(2,1)}, u32[]{:S(2)}) copy-start(bf16[256,1152]{1,0:T(8,128)(2,1)} %param.12) | copy-start | bytes 1769476
  6.5 141.3 %all-gather.3.cloned.1.call-start = ((), (), s32[]{:S(2)}) async-start(), calls=%async_computation.5 | async-start | bytes 19599360 | tf_op jit(solution)/shard_map/all_gather | solution.py:22
  9.7 10.3 %collective-permute-start.1 = (s32[256,2]{0,1:T(2,128)S(1)}, s32[256,2]{0,1:T(2,128)S(1)}, u32[]{:S(2)}, u32[]{:S(2)}) collective-permute-start(s32[256,2]{0,1:T(2,128)S(1)} %copy-done.13), channel_id=1, source_target_pairs={{0,4},{1,5},{2,6},{3,7},{4,0},{5,1},{6,2},{7,3},{8,12},{9,13},{10,... | collective-permute-start | bytes 6152 | tf_op jit(solution)/shard_map/ppermute | solution.py:88
  15.3 33.1 %all-to-all-start = ((bf16[8,32,1280]{2,1,0:T(8,128)(2,1)}), bf16[8,32,1280]{2,1,0:T(8,128)(2,1)S(1)}, u32[]{:S(2)}, u32[]{:S(2)}) async-start(bf16[8,32,1280]{2,1,0:T(8,128)(2,1)} %bitcast.205), calls=%async_computation | async-start | bytes 1310720 | tf_op jit(solution)/shard_map/all_to_all | solution.py:97
  149.1 5.9 %copy-start.9 = (f32[2560]{0:T(1024)S(1)}, f32[2560]{0:T(1024)}, u32[]{:S(2)}) copy-start(f32[2560]{0:T(1024)} %param.16) | copy-start | bytes 30724
  166.5 1.4 copy-start.1
  168.0 10.0 %copy-start.10 = (f32[2560]{0:T(1024)S(1)}, f32[2560]{0:T(1024)}, u32[]{:S(2)}) copy-start(f32[2560]{0:T(1024)} %param.18) | copy-start | bytes 30724
  178.3 3.1 copy-start.3
  179.0 2.4 copy-start.5
  181.4 63.9 %all-to-all-start.1 = ((bf16[4,1,128,2560]{3,2,1,0:T(8,128)(2,1)}), bf16[4,1,128,2560]{3,2,1,0:T(8,128)(2,1)}, u32[]{:S(2)}, u32[]{:S(2)}) async-start(bf16[4,1,128,2560]{3,2,1,0:T(8,128)(2,1)} %bitcast.199), calls=%async_computation.1 | async-start | bytes 5242880 | tf_op jit(solution)/shard_map/all_to_all | solution.py:123
  186.0 57.2 %collective-permute-start = (bf16[256,2560]{1,0:T(8,128)(2,1)}, bf16[256,2560]{1,0:T(8,128)(2,1)}, u32[]{:S(2)}, u32[]{:S(2)}) collective-permute-start(bf16[256,2560]{1,0:T(8,128)(2,1)} %copy-done.5), channel_id=1, source_target_pairs={{0,4},{1,5},{2,6},{3,7},{4,0},{5,1},{6,2},{7,3},{8,12},{9,13},{10,... | collective-permute-start | bytes 3932168 | tf_op jit(solution)/shard_map/ppermute | solution.py:164
  247.5 35.9 %copy-start.17 = (bf16[1,2560,512]{2,1,0:T(8,128)(2,1)S(1)}, bf16[1,2560,512]{2,1,0:T(8,128)(2,1)}, u32[]{:S(2)}) copy-start(bf16[1,2560,512]{2,1,0:T(8,128)(2,1)} %param.21) | copy-start | bytes 7864324
  281.9 1.6 copy-start.7
  293.3 33.2 %all-to-all-start.4 = ((bf16[4,1,128,2560]{3,2,1,0:T(8,128)(2,1)}), bf16[4,1,128,2560]{3,2,1,0:T(8,128)(2,1)}, u32[]{:S(2)}, u32[]{:S(2)}) async-start(bf16[4,1,128,2560]{3,2,1,0:T(8,128)(2,1)} %fusion.4), calls=%async_computation.4 | async-start | bytes 5242880 | tf_op jit(solution)/shard_map/all_to_all | solution.py:123
  310.3 22.0 %copy-start.8 = (bf16[2560,8]{0,1:T(8,128)(2,1)S(1)}, bf16[2560,8]{0,1:T(8,128)(2,1)}, u32[]{:S(2)}) copy-start(bf16[2560,8]{0,1:T(8,128)(2,1)} %param.20) | copy-start | bytes 122884
  310.3 23.7 %copy-start.16 = (s32[256,2]{0,1:T(2,128)S(1)}, s32[256,2]{0,1:T(2,128)}, u32[]{:S(2)}) copy-start(s32[256,2]{0,1:T(2,128)} %copy-done.15) | copy-start | bytes 6148
  326.4 55.4 %all-to-all-start.2 = ((bf16[4,1,128,2560]{3,2,1,0:T(8,128)(2,1)}), bf16[4,1,128,2560]{3,2,1,0:T(8,128)(2,1)}, u32[]{:S(2)}, u32[]{:S(2)}) async-start(bf16[4,1,128,2560]{3,2,1,0:T(8,128)(2,1)} %fusion.3), calls=%async_computation.2 | async-start | bytes 5242880 | tf_op jit(solution)/shard_map/all_to_all | solution.py:123
  336.7 7.0 %copy-start.6 = (bf16[256,2560]{1,0:T(8,128)(2,1)S(1)}, bf16[256,2560]{1,0:T(8,128)(2,1)}, u32[]{:S(2)}) copy-start(bf16[256,2560]{1,0:T(8,128)(2,1)} %copy-done.5) | copy-start | bytes 3932164
  336.7 7.5 %copy-start.14 = (s32[256,2]{0,1:T(2,128)S(1)}, s32[256,2]{0,1:T(2,128)}, u32[]{:S(2)}) copy-start(s32[256,2]{0,1:T(2,128)} %param.14) | copy-start | bytes 6148
  340.6 59.1 %collective-permute-start.2 = (bf16[256,2560]{1,0:T(8,128)(2,1)}, bf16[256,2560]{1,0:T(8,128)(2,1)}, u32[]{:S(2)}, u32[]{:S(2)}) collective-permute-start(bf16[256,2560]{1,0:T(8,128)(2,1)} %fusion.5), channel_id=1, source_target_pairs={{0,4},{1,5},{2,6},{3,7},{4,0},{5,1},{6,2},{7,3},{8,12},{9,13},{10,... | collective-permute-start | bytes 3932168 | tf_op jit(solution)/shard_map/ppermute | solution.py:169
  381.8 17.9 %copy-start.4 = (bf16[256,2560]{1,0:T(8,128)(2,1)S(1)}, bf16[256,2560]{1,0:T(8,128)(2,1)}, u32[]{:S(2)}) copy-start(bf16[256,2560]{1,0:T(8,128)(2,1)} %copy-done.3) | copy-start | bytes 3932164
  (3 other events, 2.5 us)
Sparse Core Ops, SparseCore 0:
  10.2 137.6 all-gather.2
